TPU v7x, 512 devices: a whole 4x4x16 slice. The times are simulated.
512 devices in a mesh: dp: 8 (over z_lo), expert: 8 (over x, z_hi), tensor: 8 (over y, core).
Axes of the slice: x: 4, y: 4, z: 16 (z_hi: 2, z_lo: 8; z = z_hi * 8 + z_lo), core: 2. Of those that a mesh axis runs over, the one named last changes fastest.
Arguments:
- tokens: bfloat16 [4096, 3072], P(('dp', 'expert', 'tensor')), parts along dimension 0, may hold values from -6 to 6
- expert_ids: int32 [4096, 2], P(('dp', 'expert', 'tensor')), parts along dimension 0, may hold values from 0 to 7, all different within a row; in each aligned block of 8 rows (0 to 7, 8 to 15, ...) at most 4 rows name the same one
- gate_weights: float32 [4096, 2], P(('dp', 'expert', 'tensor')), parts along dimension 0, may hold values from 0.2 to 1
- gate_proj: bfloat16 [8, 3072, 8192], P('expert', None, 'tensor'), may hold values from -0.109375 to 0.109375
- up_proj: bfloat16 [8, 3072, 8192], P('expert', None, 'tensor'), may hold values from -0.109375 to 0.109375
- down_proj: bfloat16 [8, 8192, 3072], P('expert', 'tensor'), may hold values from -0.0625 to 0.0625
Outputs:
- mixture: bfloat16 [4096, 3072], P(('dp', 'expert', 'tensor')), parts along dimension 0
There are 8 independent parts, one for each index of `dp`. A program takes and returns all parts, laid end to end along the dimension named above; an argument that names none is the same for every part. Nothing has to cross between parts.
Inputs may be any that keep to these rules, and one draw needn't show every extreme that they name: `expert_ids`: each token names two different experts; no expert is named by more than 4 tokens of one device (aligned blocks of 8 rows), and some blocks reach this bound.
All inputs are finite; a program needn't handle non-finite values.
Results may differ from a plain program's by a relative error of at most 0.015.
Values may be sent and summed in bfloat16 or wider, within the bound.
No kernel may reach another device: no remote copies, remote signals or barrier semaphores. Data moves between devices by JAX's collectives and lax.ppermute only.
A program may use at most 64 MiB of HBM per device.

v0:
```python
import jax
import jax.numpy as jnp
from jax import lax
from jax.sharding import PartitionSpec as P


def sent_to_all(shard, axis):
    devices = lax.axis_size(axis)
    return lax.all_to_all(
        jnp.broadcast_to(shard[None], (devices, *shard.shape)), axis, 0, 0, tiled=True
    )


def laid_out(parts, dim):
    parts = jnp.moveaxis(parts, 0, dim)
    dims = parts.shape
    return parts.reshape(*dims[:dim], dims[dim] * dims[dim + 1], *dims[dim + 2 :])


def gathered_copies(shard, axis, dim):
    parts = sent_to_all(shard, axis)
    return laid_out(parts, dim)


def cut_along(shard, dim, devices):
    dims = shard.shape
    parts = shard.reshape(*dims[:dim], devices, dims[dim] // devices, *dims[dim + 1 :])
    return jnp.moveaxis(parts, dim, 0)


def sent_and_summed(shard, axis, dim):
    devices = lax.axis_size(axis)
    parts = lax.all_to_all(cut_along(shard, dim, devices), axis, 0, 0, tiled=True)
    return jnp.sum(parts.astype(jnp.float32), axis=0)


def expert_rows(rows, w_gate, w_up, w_down):
    width = rows.shape[-1]
    flat = rows.reshape(-1, width)
    gate = jnp.dot(flat, w_gate, preferred_element_type=jnp.float32)
    upward = jnp.dot(flat, w_up, preferred_element_type=jnp.float32)
    hidden = (jax.nn.silu(gate) * upward).astype(jnp.bfloat16)
    output = jnp.dot(hidden, w_down, preferred_element_type=jnp.float32).astype(jnp.bfloat16)
    return output.reshape(rows.shape[:-1] + (w_down.shape[1],))


def on_device(tokens, expert_ids, gate_weights, gate_proj, up_proj, down_proj):
    experts = lax.axis_size("expert")
    local_rows, width = tokens.shape
    capacity = min(local_rows, 4 * local_rows // experts)
    w_gate = gate_proj[0]
    w_up = up_proj[0]
    w_down = down_proj[0]
    flat_ids = expert_ids.reshape(-1)
    onehot = (flat_ids[:, None] == jnp.arange(experts, dtype=jnp.int32)[None, :]).astype(jnp.int32)
    earlier = jnp.cumsum(onehot, axis=0) - onehot
    slots = jnp.sum(onehot * earlier, axis=1)
    target = flat_ids * capacity + slots
    placed = target[:, None] == jnp.arange(experts * capacity, dtype=jnp.int32)[None, :]
    doubled = jnp.repeat(tokens, 2, axis=0)
    outgoing = jnp.dot(placed.astype(jnp.bfloat16).T, doubled, preferred_element_type=jnp.float32)
    outgoing = outgoing.astype(jnp.bfloat16).reshape(experts, capacity, width)
    arrived = lax.all_to_all(outgoing, "expert", split_axis=0, concat_axis=0, tiled=True)
    partials = expert_rows(gathered_copies(arrived[:, None], "tensor", 1), w_gate, w_up, w_down)
    summed = sent_and_summed(partials.astype(jnp.float32).astype(jnp.bfloat16), "tensor", 1)
    results = lax.all_to_all(
        summed[:, 0].astype(jnp.bfloat16), "expert", split_axis=0, concat_axis=0, tiled=True
    )
    weights = placed.astype(jnp.float32) * gate_weights.reshape(-1)[:, None]
    contrib = jnp.dot(
        weights,
        results.reshape(experts * capacity, width).astype(jnp.float32),
        precision=lax.Precision.HIGHEST,
    )
    return contrib.reshape(local_rows, 2, width).sum(axis=1).astype(jnp.bfloat16)


def solution(mesh):
    return jax.shard_map(
        on_device,
        mesh=mesh,
        in_specs=(
            P(("dp", "expert", "tensor"), None),
            P(("dp", "expert", "tensor"), None),
            P(("dp", "expert", "tensor"), None),
            P("expert", None, "tensor"),
            P("expert", None, "tensor"),
            P("expert", "tensor", None),
        ),
        out_specs=P(("dp", "expert", "tensor"), None),
        check_vma=False,
    )
```

profile of v0, /device:TPU:33, one launch (start us, length us, event | category | flops | bytes accessed | tf_op | source)
XLA Modules:
  0.0 132.4 jit_solution(6869242384580702733)
XLA Ops:
  0.0 0.8 copy.13
  0.8 0.1 eq.48
  0.8 0.1 fusion.20
  0.9 0.2 select_reduce_fusion
  1.1 0.9 broadcast_in_dim.4
  2.0 0.3 convolution_convert_fusion
  2.4 0.1 reshape.63
  2.5 37.0 %all_to_all.20 = bf16[8,4,3072]{2,1,0:T(4,128)(2,1)S(1)} all-to-all(bf16[8,4,3072]{2,1,0:T(4,128)(2,1)S(1)} %reshape.63), channel_id=1, replica_groups=mesh['dp'=8,'expert'=8,'tensor'=8] {'expert'}, dimensions={0} | all-to-all | bytes 393216 | tf_op jit(solution)/shard_map/all_to_all | solution.py:63
  39.4 0.5 broadcast_in_dim.5
  40.0 26.8 %all_to_all.21 = bf16[8,8,1,4,3072]{4,3,1,2,0:T(4,128)(2,1)S(1)} all-to-all(bf16[8,8,1,4,3072]{4,3,1,2,0:T(4,128)(2,1)S(1)} %broadcast_in_dim.5), channel_id=1, replica_groups=mesh['dp'=8,'expert'=8,'tensor'=8] {'tensor'}, dimensions={0} | all-to-all | bytes 3145728 | tf_op jit(solution)/shard_map/all_to_all | solution.py:9
  66.8 0.6 copy.16
  67.4 0.4 reshape_reshape.3
  67.8 5.6 %fusion.4 = f32[256,1024]{1,0:T(8,128)} fusion(bf16[256,3072]{1,0:T(8,128)(2,1)S(1)} %reshape_reshape.3, bf16[1,3072,1024]{2,1,0:T(8,128)(2,1)} %param.9), kind=kOutput, calls=%fused_computation.4 | convolution fusion | flops 1610612736 | bytes 8912896 | tf_op jit(solution)/shard_map/dot_general | solution.py:40
  73.4 8.5 %fusion.6 = bf16[256,3072]{1,0:T(8,128)(2,1)S(1)} fusion(bf16[1,1024,3072]{2,1,0:T(8,128)(2,1)} %param.11, bf16[256,3072]{1,0:T(8,128)(2,1)S(1)} %reshape_reshape.3, bf16[1,3072,1024]{2,1,0:T(8,128)(2,1)} %param.10, f32[256,1024]{1,0:T(8,128)} %fusion.4), kind=kOutput, calls=%fused_computation.6 | convolution fusion | flops 3223584768 | bytes 16777216 | tf_op jit(solution)/shard_map/dot_general | solution.py:43
  81.9 0.6 reshape.64
  82.5 0.6 copy.19
  83.2 24.2 %all_to_all.22 = bf16[8,8,1,4,3072]{4,3,1,2,0:T(4,128)(2,1)S(1)} all-to-all(bf16[8,8,1,4,3072]{4,3,1,2,0:T(4,128)(2,1)S(1)} %bitcast.31), channel_id=1, replica_groups=mesh['dp'=8,'expert'=8,'tensor'=8] {'tensor'}, dimensions={0} | all-to-all | bytes 3145728 | tf_op jit(solution)/shard_map/all_to_all | solution.py:33
  107.4 0.0 copy-start
  107.4 1.6 %reduce_sum.34 = bf16[8,4,3072]{2,1,0:T(4,128)(2,1)} reduce(bf16[8,8,1,4,3072]{4,3,1,2,0:T(4,128)(2,1)S(1)} %all_to_all.22, bf16[]{:T(256)} %constant.15.clone.1), dimensions={0,2}, to_apply=%region_2.3 | reduce | flops 688128 | bytes 1769474 | tf_op jit(solution)/shard_map/reduce_sum | solution.py:34
  109.0 3.4 %all-to-all-start.3 = ((bf16[8,4,3072]{2,1,0:T(4,128)(2,1)}), bf16[8,4,3072]{2,1,0:T(4,128)(2,1)S(1)}, u32[]{:S(2)}, u32[]{:S(2)}) async-start(bf16[8,4,3072]{2,1,0:T(4,128)(2,1)} %reduce_sum.34), calls=%async_computation.3 | async-start | bytes 393216 | tf_op jit(solution)/shard_map/all_to_all | solution.py:66
  112.4 0.1 reduce_sum.33
  112.5 0.1 copy.15
  112.6 18.9 %all-to-all-done.3 = bf16[8,4,3072]{2,1,0:T(4,128)(2,1)S(1)} async-done(((bf16[8,4,3072]{2,1,0:T(4,128)(2,1)}), bf16[8,4,3072]{2,1,0:T(4,128)(2,1)S(1)}, u32[]{:S(2)}, u32[]{:S(2)}) %all-to-all-start.3) | async-done | bytes 196640 | tf_op jit(solution)/shard_map/all_to_all | solution.py:66
  131.5 0.0 copy-done
  131.5 0.9 convolution_reduce_fusion
  (5 shorter events, 0.1 us)
Async XLA Ops:
  107.4 24.1 %copy-start = (f32[8,2]{0,1:T(2,128)S(1)}, f32[8,2]{0,1:T(2,128)}, u32[]{:S(2)}) copy-start(f32[8,2]{0,1:T(2,128)} %param.8) | copy-start | bytes 196
  109.0 22.5 %all-to-all-start.3 = ((bf16[8,4,3072]{2,1,0:T(4,128)(2,1)}), bf16[8,4,3072]{2,1,0:T(4,128)(2,1)S(1)}, u32[]{:S(2)}, u32[]{:S(2)}) async-start(bf16[8,4,3072]{2,1,0:T(4,128)(2,1)} %reduce_sum.34), calls=%async_computation.3 | async-start | bytes 393216 | tf_op jit(solution)/shard_map/all_to_all | solution.py:66
where the time goes:
time: 133 us; the launch traced here: 132 us
  blocking collectives  88 us (66%)
  waiting for transfers between devices  18.9 us (14%)
  matrix products  15.4 us (12%)
  local copies, waits for them, and re-layouts  4.77 us (4%)
  starting transfers between devices  3.39 us (3%)
  other arithmetic  1.89 us (1%)
    all_to_all x1, blocking collectives, on_device(): lax.all_to_all(outgoing, 'expert', split_axis=0, concat_axis=0, tiled=True)  37 us
    all_to_all x1, blocking collectives, sent_to_all(): lax.all_to_all(jnp.broadcast_to(shard[None], (devices, *shard.shape)), ax...  26.8 us
    all_to_all x1, blocking collectives, sent_and_summed(): lax.all_to_all(cut_along(shard, dim, devices), axis, 0, 0, tiled=True)  24.2 us
    all_to_all x1, waiting for transfers between devices, on_device(): lax.all_to_all(summed[:, 0].astype(jnp.bfloat16), 'expert', split_axis=0,...  18.9 us
    dot_general x1, matrix products, expert_rows(): jnp.dot(hidden, w_down, preferred_element_type=jnp.float32)  8.51 us
    dot_general x1, matrix products, expert_rows(): gate = jnp.dot(flat, w_gate, preferred_element_type=jnp.float32)  5.62 us
    all_to_all x1, starting transfers between devices, on_device(): lax.all_to_all(summed[:, 0].astype(jnp.bfloat16), 'expert', split_axis=0,...  3.39 us
  transfers between devices with their start and end apart: 1, of which 1 were waited for; matrix products, arithmetic and copies ran while one was open for 0% of the time, Pallas kernels for 0%

commit v1 on v0

v1 whole, which is shorter than its diff:
```python
import functools

import jax
import jax.numpy as jnp
from jax import lax
from jax.experimental import pallas as pl
from jax.experimental.pallas import tpu as pltpu
from jax.sharding import Mesh, PartitionSpec as P

X, ZH, Y, CORE = 4, 2, 4, 2
SLOTS = 4
META = 128
BF16, F32 = jnp.bfloat16, jnp.float32
VMEM = pltpu.MemorySpace.VMEM
SMEM = pltpu.MemorySpace.SMEM


def dot(a, b, contract=((1,), (0,))):
    return lax.dot_general(a, b, (contract, ((), ())), preferred_element_type=F32)


def iota(shape, dim):
    return lax.broadcasted_iota(jnp.int32, shape, dim)


def pack_kernel(tok_ref, ids_ref, gw_ref, out_ref, meta_ref):
    rows, width = tok_ref.shape
    out_ref[:, :width] = tok_ref[...]
    w = gw_ref[...]
    high = w.astype(BF16).astype(F32)
    mid = (w - high).astype(BF16).astype(F32)
    meta_ref[...] = jnp.zeros(meta_ref.shape, F32)
    meta_ref[0:2, 0:rows] = ids_ref[...].astype(F32)
    meta_ref[2:4, 0:rows] = high
    meta_ref[4:6, 0:rows] = mid
    meta_ref[6:8, 0:rows] = w - high - mid
    out_ref[:, width:] = meta_ref[...].astype(BF16)


def packed(tokens, ids, gate_weights):
    rows, width = tokens.shape
    return pl.pallas_call(
        pack_kernel,
        out_shape=jax.ShapeDtypeStruct((rows, width + META), BF16),
        scratch_shapes=[pltpu.VMEM((8, META), F32)],
        name="pack",
    )(tokens, ids.T, gate_weights.T)


def placement(meta, zh, block):
    rows = 8
    meta = meta.astype(F32)
    r = iota((X * 2 * SLOTS, rows), 0)
    expert = ((r // (2 * SLOTS)) * ZH + zh).astype(F32)
    named = jnp.where((meta[0:1, :rows] == expert) | (meta[1:2, :rows] == expert), 1.0, 0.0)
    before = jnp.where(iota((rows, rows), 0) < iota((rows, rows), 1), 1.0, 0.0)
    rank = dot(named.astype(BF16), before.astype(BF16))
    mine = (r // SLOTS) % 2 == block
    return jnp.where(mine & (named > 0.5) & (rank == (r % SLOTS).astype(F32)), 1.0, 0.0).astype(BF16)


def place_kernel(zh_ref, own_ref, other_ref, out_ref):
    width = out_ref.shape[-1]
    zh = zh_ref[0]
    slots = dot(placement(own_ref[:, width:], zh, 0), own_ref[:, :width])
    slots = slots + dot(placement(other_ref[:, width:], zh, 1), other_ref[:, :width])
    slots = slots.astype(BF16)
    for x in range(X):
        for y in range(Y):
            out_ref[x * Y + y] = slots[x * 2 * SLOTS : (x + 1) * 2 * SLOTS]


def placed(zh, own, other):
    width = own.shape[1] - META
    return pl.pallas_call(
        place_kernel,
        out_shape=jax.ShapeDtypeStruct((X * Y, 2 * SLOTS, width), BF16),
        in_specs=[pl.BlockSpec(memory_space=SMEM), pl.BlockSpec(memory_space=VMEM), pl.BlockSpec(memory_space=VMEM)],
        name="place",
    )(zh, own, other)


def ffn_kernel(a_ref, b_ref, wg_ref, wu_ref, wd_ref, pa_ref, pb_ref, rows_ref, acc_ref):
    step = pl.program_id(0)
    half = a_ref.shape[0]

    @pl.when(step == 0)
    def _():
        rows_ref[:half] = a_ref[...]
        rows_ref[half:] = b_ref[...]

    rows = rows_ref[...]
    gate = dot(rows, wg_ref[0])
    up = dot(rows, wu_ref[0])
    hidden = (gate / (1.0 + jnp.exp(-gate)) * up).astype(BF16)
    part = dot(hidden, wd_ref[0])

    @pl.when(step == 0)
    def _():
        acc_ref[...] = part

    @pl.when(step > 0)
    def _():
        acc_ref[...] += part

    @pl.when(step == pl.num_programs(0) - 1)
    def _():
        pa_ref[...] = acc_ref[:half]
        pb_ref[...] = acc_ref[half:].astype(BF16)


def ffn(a, b, wg, wu, wd, block=256):
    half, width = a.shape
    hidden = wg.shape[2]
    whole = pl.BlockSpec((half, width), lambda i: (0, 0))
    return pl.pallas_call(
        ffn_kernel,
        out_shape=(jax.ShapeDtypeStruct((half, width), F32), jax.ShapeDtypeStruct((half, width), BF16)),
        grid=(hidden // block,),
        in_specs=[
            whole,
            whole,
            pl.BlockSpec((1, width, block), lambda i: (0, 0, i)),
            pl.BlockSpec((1, width, block), lambda i: (0, 0, i)),
            pl.BlockSpec((1, block, width), lambda i: (0, i, 0)),
        ],
        out_specs=(whole, whole),
        scratch_shapes=[pltpu.VMEM((2 * half, width), BF16), pltpu.VMEM((2 * half, width), F32)],
        compiler_params=pltpu.CompilerParams(vmem_limit_bytes=48 * 2**20),
        name="ffn",
    )(a, b, wg, wu, wd)


def mixing(meta, zh, block):
    rows = 8
    eye = jnp.where(iota((8, 8), 0) == iota((8, 8), 1), 1.0, 0.0).astype(BF16)
    fields = dot(eye, meta[:, :rows], ((1,), (1,)))
    lanes = X * Y * 2 * SLOTS
    r = iota((rows, lanes), 1)
    expert = ((r // (Y * 2 * SLOTS)) * ZH + zh).astype(F32)
    first = fields[:, 0:1] == expert
    second = fields[:, 1:2] == expert
    named = jnp.where(first | second, 1.0, 0.0)
    before = jnp.where(iota((rows, rows), 1) < iota((rows, rows), 0), 1.0, 0.0)
    rank = dot(before.astype(BF16), named.astype(BF16))
    w0 = fields[:, 2:3] + fields[:, 4:5] + fields[:, 6:7]
    w1 = fields[:, 3:4] + fields[:, 5:6] + fields[:, 7:8]
    mine = (r // SLOTS) % 2 == block
    weight = jnp.where(first, w0, jnp.where(second, w1, 0.0))
    return jnp.where(mine & (rank == (r % SLOTS).astype(F32)), weight, 0.0)


def mixed(weights, rows):
    high = weights.astype(BF16)
    rest = weights - high.astype(F32)
    mid = rest.astype(BF16)
    low = (rest - mid.astype(F32)).astype(BF16)
    return dot(high, rows) + dot(mid, rows) + dot(low, rows)


def combine_kernel(zh_ref, rows_ref, own_ref, other_ref, keep_ref, send_ref):
    zh = zh_ref[0]
    rows = rows_ref[...]
    keep_ref[...] = mixed(mixing(own_ref[...], zh, 0), rows)
    send_ref[...] = mixed(mixing(other_ref[...], zh, 1), rows).astype(BF16)


def combined(zh, rows, own, other):
    width = rows.shape[1]
    meta = pl.BlockSpec((8, META), lambda i: (0, width // META))
    tokens = pl.BlockSpec((8, width), lambda i: (0, 0))
    return pl.pallas_call(
        combine_kernel,
        grid=(1,),
        out_shape=(jax.ShapeDtypeStruct((8, width), F32), jax.ShapeDtypeStruct((8, width), BF16)),
        in_specs=[pl.BlockSpec(memory_space=SMEM), pl.BlockSpec(rows.shape, lambda i: (0, 0)), meta, meta],
        out_specs=(tokens, tokens),
        name="combine",
    )(zh, rows, own, other)


def swapped(value, axis):
    return lax.ppermute(value, axis, [(0, 1), (1, 0)])


def on_device(tokens, expert_ids, gate_weights, gate_proj, up_proj, down_proj):
    width = tokens.shape[1]
    zh = lax.axis_index("zh").astype(jnp.int32).reshape(1)
    own = packed(tokens, expert_ids, gate_weights)
    other = swapped(own, "zh")
    slots = placed(zh, own, other)
    rows = lax.all_to_all(slots, ("x", "y"), 0, 0, tiled=True).reshape(-1, width)
    core_rows = swapped(rows, "core")
    part, core_part = ffn(rows, core_rows, gate_proj, up_proj, down_proj)
    pair = (part + swapped(core_part, "core").astype(F32)).astype(BF16)
    back = lax.all_to_all(pair.reshape(slots.shape), ("x", "y"), 0, 0, tiled=True)
    keep, send = combined(zh, back.reshape(-1, width), own, other)
    return (keep + swapped(send, "zh").astype(F32)).astype(BF16)


def solution(mesh):
    dp = mesh.shape["dp"]
    fine = Mesh(mesh.devices.reshape(dp, X, ZH, Y, CORE), ("dp", "x", "zh", "y", "core"))
    every = P(("dp", "x", "zh", "y", "core"), None)
    return jax.shard_map(
        on_device,
        mesh=fine,
        in_specs=(
            every,
            every,
            every,
            P(("x", "zh"), None, ("y", "core")),
            P(("x", "zh"), None, ("y", "core")),
            P(("x", "zh"), ("y", "core"), None),
        ),
        out_specs=every,
        check_vma=False,
    )
```

time: 133 us -> 99.3 us (0.75)
  the two profiles are of different devices: /device:TPU:33 before, /device:TPU:192 now
where the time goes in v1:
time: 99.3 us; the launch traced here: 98.9 us
  blocking collectives  39.8 us (40%)
  waiting for transfers between devices  20.7 us (21%)
  starting transfers between devices  18.9 us (19%)
  Pallas kernels  17.1 us (17%)
  other arithmetic  1.68 us (2%)
    all_to_all x1, blocking collectives, on_device(): lax.all_to_all(slots, ('x', 'y'), 0, 0, tiled=True).reshape(-1, width)  21.8 us
    ppermute x4, waiting for transfers between devices, swapped(): return lax.ppermute(value, axis, [(0, 1), (1, 0)])  20.7 us
    ppermute x4, starting transfers between devices, swapped(): return lax.ppermute(value, axis, [(0, 1), (1, 0)])  18.9 us
    all_to_all x1, blocking collectives, on_device(): lax.all_to_all(pair.reshape(slots.shape), ('x', 'y'), 0, 0, tiled=True)  18 us
    pallas_call x1, Pallas kernels, ffn(): pl.pallas_call(ffn_kernel, out_shape=(jax.ShapeDtypeStruct((half, width),...  10.5 us
    pallas_call x1, Pallas kernels, combined(): pl.pallas_call(combine_kernel, grid=(1,), out_shape=(jax.ShapeDtypeStruct...  3.07 us
    pallas_call x1, Pallas kernels, placed(): pl.pallas_call(place_kernel, out_shape=jax.ShapeDtypeStruct((X * Y, 2 * S...  2.09 us
  transfers between devices with their start and end apart: 4, of which 4 were waited for; matrix products, arithmetic and copies ran while one was open for 0% of the time, Pallas kernels for 0%

profile of v1, /device:TPU:192, one launch (start us, length us, event | category | flops | bytes accessed | tf_op | source)
XLA Modules:
  0.0 98.9 jit_solution(7034176505961294304)
XLA Ops:
  0.0 1.5 %pack.1.own_ref = bf16[8,3200]{1,0:T(8,128)(2,1)} custom-call(bf16[8,3072]{1,0:T(8,128)(2,1)} %tok_ref.1, s32[2,8]{1,0:T(2,128)} %bitcast.10, f32[2,8]{1,0:T(2,128)} %bitcast.11), custom_call_target="tpu_custom_call" | custom-call | tf_op jit(solution)/shard_map/pack/pallas_call | solution.py:42
  1.5 9.1 %collective-permute-start = (bf16[8,3200]{1,0:T(8,128)(2,1)}, bf16[8,3200]{1,0:T(8,128)(2,1)S(1)}, u32[]{:S(2)}, u32[]{:S(2)}) collective-permute-start(bf16[8,3200]{1,0:T(8,128)(2,1)} %pack.1.own_ref), channel_id=1, source_target_pairs={{0,8},{8,0},{1,9},{9,1},{2,10},{10,2},{3,11},{11,3},{4,12},{12,4},... | collective-permute-start | bytes 153608 | tf_op jit(solution)/shard_map/ppermute | solution.py:183
  10.6 7.3 %collective-permute-done.other_ref = bf16[8,3200]{1,0:T(8,128)(2,1)S(1)} collective-permute-done((bf16[8,3200]{1,0:T(8,128)(2,1)}, bf16[8,3200]{1,0:T(8,128)(2,1)S(1)}, u32[]{:S(2)}, u32[]{:S(2)}) %collective-permute-start) | collective-permute-done | bytes 51232 | tf_op jit(solution)/shard_map/ppermute | solution.py:183
  17.8 0.0 copy-start
  17.8 0.6 copy-done
  18.5 2.1 %place.1 = bf16[16,8,3072]{2,1,0:T(8,128)(2,1)} custom-call(s32[1]{0:T(128)} %bitcast.zh_ref, bf16[8,3200]{1,0:T(8,128)(2,1)} %pack.1.own_ref, bf16[8,3200]{1,0:T(8,128)(2,1)} %copy-done), custom_call_target="tpu_custom_call" | custom-call | tf_op jit(solution)/shard_map/place/pallas_call | solution.py:75
  20.5 21.8 %all_to_all.10 = bf16[16,8,3072]{2,1,0:T(8,128)(2,1)S(1)} all-to-all(bf16[16,8,3072]{2,1,0:T(8,128)(2,1)} %place.1), channel_id=1, replica_groups=mesh['dp'=8,'x'=4,'zh'=2,'y'=4,'core'=2] {'x','y'}, dimensions={0} | all-to-all | bytes 1572864 | tf_op jit(solution)/shard_map/all_to_all | solution.py:192
  42.3 1.9 %collective-permute-start.1 = (bf16[128,3072]{1,0:T(8,128)(2,1)S(1)}, bf16[128,3072]{1,0:T(8,128)(2,1)S(1)}, u32[]{:S(2)}, u32[]{:S(2)}) collective-permute-start(bf16[128,3072]{1,0:T(8,128)(2,1)S(1)} %bitcast.7), channel_id=1, source_target_pairs={{0,1},{1,0},{2,3},{3,2},{4,5},{5,4},{6,7},{7,6},{8,9},{9,8},{10,11... | collective-permute-start | bytes 2359304 | tf_op jit(solution)/shard_map/ppermute | solution.py:183
  44.2 2.3 %collective-permute-done.1.b_ref = bf16[128,3072]{1,0:T(8,128)(2,1)S(1)} collective-permute-done((bf16[128,3072]{1,0:T(8,128)(2,1)S(1)}, bf16[128,3072]{1,0:T(8,128)(2,1)S(1)}, u32[]{:S(2)}, u32[]{:S(2)}) %collective-permute-start.1) | collective-permute-done | bytes 786464 | tf_op jit(solution)/shard_map/ppermute | solution.py:183
  46.5 10.5 %ffn.1 = (f32[128,3072]{1,0:T(8,128)S(1)}, bf16[128,3072]{1,0:T(8,128)(2,1)S(1)}) custom-call(bf16[128,3072]{1,0:T(8,128)(2,1)S(1)} %bitcast.8, bf16[128,3072]{1,0:T(8,128)(2,1)S(1)} %collective-permute-done.1.b_ref, bf16[1,3072,1024]{2,1,0:T(8,128)(2,1)} %wg_ref.1, bf16[1,3072,1024]{2,1,0:T(8,128)(2,1)} %wu_ref.1, bf16[1,1024,3072]{2,1,0:T(8,128)(2,1)} %wd_ref.1), custom_call_target="tpu_custom_call" | custom-call | tf_op jit(solution)/shard_map/ffn/pallas_call | solution.py:116
  57.0 2.0 %collective-permute-start.2 = (bf16[128,3072]{1,0:T(8,128)(2,1)S(1)}, bf16[128,3072]{1,0:T(8,128)(2,1)S(1)}, u32[]{:S(2)}, u32[]{:S(2)}) collective-permute-start(bf16[128,3072]{1,0:T(8,128)(2,1)S(1)} %get-tuple-element.10), channel_id=1, source_target_pairs={{0,1},{1,0},{2,3},{3,2},{4,5},{5,4},{6,7},{7,6},{8,9},{9,8},{10,11... | collective-permute-start | bytes 2359304 | tf_op jit(solution)/shard_map/ppermute | solution.py:183
  59.1 2.1 %collective-permute-done.2 = bf16[128,3072]{1,0:T(8,128)(2,1)S(1)} collective-permute-done((bf16[128,3072]{1,0:T(8,128)(2,1)S(1)}, bf16[128,3072]{1,0:T(8,128)(2,1)S(1)}, u32[]{:S(2)}, u32[]{:S(2)}) %collective-permute-start.2) | collective-permute-done | bytes 786464 | tf_op jit(solution)/shard_map/ppermute | solution.py:183
  61.2 0.1 fusion
  61.4 18.0 %all_to_all.11 = bf16[16,8,3072]{2,1,0:T(8,128)(2,1)} all-to-all(bf16[16,8,3072]{2,1,0:T(8,128)(2,1)S(1)} %fusion), channel_id=1, replica_groups=mesh['dp'=8,'x'=4,'zh'=2,'y'=4,'core'=2] {'x','y'}, dimensions={0} | all-to-all | bytes 1572864 | tf_op jit(solution)/shard_map/all_to_all | solution.py:196
  79.4 3.1 %combine.1 = (f32[8,3072]{1,0:T(8,128)}, bf16[8,3072]{1,0:T(8,128)(2,1)}) custom-call(s32[1]{0:T(128)} %bitcast.zh_ref, bf16[128,3072]{1,0:T(8,128)(2,1)} %bitcast.9, bf16[8,3200]{1,0:T(8,128)(2,1)} %pack.1.own_ref, bf16[8,3200]{1,0:T(8,128)(2,1)} %copy-done), custom_call_target="tpu_custom_call" | custom-call | tf_op jit(solution)/shard_map/combine/pallas_call | solution.py:172
  82.4 5.8 %collective-permute-start.3 = (bf16[8,3072]{1,0:T(8,128)(2,1)}, bf16[8,3072]{1,0:T(8,128)(2,1)S(1)}, u32[]{:S(2)}, u32[]{:S(2)}) collective-permute-start(bf16[8,3072]{1,0:T(8,128)(2,1)} %get-tuple-element.12), channel_id=1, source_target_pairs={{0,8},{8,0},{1,9},{9,1},{2,10},{10,2},{3,11},{11,3},{4,12},{12,4},... | collective-permute-start | bytes 147464 | tf_op jit(solution)/shard_map/ppermute | solution.py:183
  88.3 9.1 %collective-permute-done.3 = bf16[8,3072]{1,0:T(8,128)(2,1)S(1)} collective-permute-done((bf16[8,3072]{1,0:T(8,128)(2,1)}, bf16[8,3072]{1,0:T(8,128)(2,1)S(1)}, u32[]{:S(2)}, u32[]{:S(2)}) %collective-permute-start.3) | collective-permute-done | bytes 49184 | tf_op jit(solution)/shard_map/ppermute | solution.py:183
  97.3 1.5 %add_convert_fusion.1 = bf16[8,3072]{1,0:T(8,128)(2,1)} fusion(f32[8,3072]{1,0:T(8,128)} %get-tuple-element.11, bf16[8,3072]{1,0:T(8,128)(2,1)S(1)} %collective-permute-done.3), kind=kLoop, calls=%fused_computation.2 | loop fusion | flops 73728 | bytes 196608 | tf_op jit(solution)/shard_map/convert_element_type | solution.py:198
Async XLA Ops:
  1.5 16.4 %collective-permute-start = (bf16[8,3200]{1,0:T(8,128)(2,1)}, bf16[8,3200]{1,0:T(8,128)(2,1)S(1)}, u32[]{:S(2)}, u32[]{:S(2)}) collective-permute-start(bf16[8,3200]{1,0:T(8,128)(2,1)} %pack.1.own_ref), channel_id=1, source_target_pairs={{0,8},{8,0},{1,9},{9,1},{2,10},{10,2},{3,11},{11,3},{4,12},{12,4},... | collective-permute-start | bytes 153608 | tf_op jit(solution)/shard_map/ppermute | solution.py:183
  17.8 0.6 copy-start
  42.3 4.2 %collective-permute-start.1 = (bf16[128,3072]{1,0:T(8,128)(2,1)S(1)}, bf16[128,3072]{1,0:T(8,128)(2,1)S(1)}, u32[]{:S(2)}, u32[]{:S(2)}) collective-permute-start(bf16[128,3072]{1,0:T(8,128)(2,1)S(1)} %bitcast.7), channel_id=1, source_target_pairs={{0,1},{1,0},{2,3},{3,2},{4,5},{5,4},{6,7},{7,6},{8,9},{9,8},{10,11... | collective-permute-start | bytes 2359304 | tf_op jit(solution)/shard_map/ppermute | solution.py:183
  57.0 4.2 %collective-permute-start.2 = (bf16[128,3072]{1,0:T(8,128)(2,1)S(1)}, bf16[128,3072]{1,0:T(8,128)(2,1)S(1)}, u32[]{:S(2)}, u32[]{:S(2)}) collective-permute-start(bf16[128,3072]{1,0:T(8,128)(2,1)S(1)} %get-tuple-element.10), channel_id=1, source_target_pairs={{0,1},{1,0},{2,3},{3,2},{4,5},{5,4},{6,7},{7,6},{8,9},{9,8},{10,11... | collective-permute-start | bytes 2359304 | tf_op jit(solution)/shard_map/ppermute | solution.py:183
  82.4 14.9 %collective-permute-start.3 = (bf16[8,3072]{1,0:T(8,128)(2,1)}, bf16[8,3072]{1,0:T(8,128)(2,1)S(1)}, u32[]{:S(2)}, u32[]{:S(2)}) collective-permute-start(bf16[8,3072]{1,0:T(8,128)(2,1)} %get-tuple-element.12), channel_id=1, source_target_pairs={{0,8},{8,0},{1,9},{9,1},{2,10},{10,2},{3,11},{11,3},{4,12},{12,4},... | collective-permute-start | bytes 147464 | tf_op jit(solution)/shard_map/ppermute | solution.py:183

commit v2 on v1

v2 whole, which is shorter than its diff:
```python
import functools

import jax
import jax.numpy as jnp
from jax import lax
from jax.experimental import pallas as pl
from jax.experimental.pallas import tpu as pltpu
from jax.sharding import Mesh, PartitionSpec as P

X, ZH, Y, CORE = 4, 2, 4, 2
SLOTS = 4
META = 128
BF16, F32 = jnp.bfloat16, jnp.float32
VMEM = pltpu.MemorySpace.VMEM
SMEM = pltpu.MemorySpace.SMEM


def dot(a, b, contract=((1,), (0,))):
    return lax.dot_general(a, b, (contract, ((), ())), preferred_element_type=F32)


def iota(shape, dim):
    return lax.broadcasted_iota(jnp.int32, shape, dim)


def call(kernel, outs, args, name, scratch=(), limit=4 * 2**20):
    specs = [pl.BlockSpec(memory_space=SMEM if a.size == 1 else VMEM) for a in args]
    args = [a if a.size == 1 else pltpu.with_memory_space_constraint(a, VMEM) for a in args]
    return pl.pallas_call(
        kernel,
        out_shape=tuple(VMEM(shape, dtype) for shape, dtype in outs),
        in_specs=specs,
        out_specs=tuple(pl.BlockSpec(memory_space=VMEM) for _ in outs),
        scratch_shapes=scratch,
        compiler_params=pltpu.CompilerParams(vmem_limit_bytes=limit),
        name=name,
    )(*args)


def in_hbm(*arrays):
    return [pltpu.with_memory_space_constraint(a, pltpu.MemorySpace.HBM) for a in arrays]


def pack_kernel(tok_ref, ids_ref, gw_ref, out_ref, meta_ref):
    rows, width = tok_ref.shape
    out_ref[:, :width] = tok_ref[...]
    w = gw_ref[...]
    high = w.astype(BF16).astype(F32)
    mid = (w - high).astype(BF16).astype(F32)
    meta_ref[...] = jnp.zeros(meta_ref.shape, F32)
    meta_ref[0:2, 0:rows] = ids_ref[...].astype(F32)
    meta_ref[2:4, 0:rows] = high
    meta_ref[4:6, 0:rows] = mid
    meta_ref[6:8, 0:rows] = w - high - mid
    out_ref[:, width:] = meta_ref[...].astype(BF16)


def packed(tokens, ids, gate_weights):
    rows, width = tokens.shape
    return pl.pallas_call(
        pack_kernel,
        out_shape=VMEM((rows, width + META), BF16),
        out_specs=pl.BlockSpec(memory_space=VMEM),
        scratch_shapes=[pltpu.VMEM((8, META), F32)],
        compiler_params=pltpu.CompilerParams(vmem_limit_bytes=2**20),
        name="pack",
    )(*in_hbm(tokens, ids.T, gate_weights.T))


def placement(meta, zh, block):
    rows = 8
    meta = meta.astype(F32)
    r = iota((X * 2 * SLOTS, rows), 0)
    expert = ((r // (2 * SLOTS)) * ZH + zh).astype(F32)
    named = jnp.where((meta[0:1, :rows] == expert) | (meta[1:2, :rows] == expert), 1.0, 0.0)
    before = jnp.where(iota((rows, rows), 0) < iota((rows, rows), 1), 1.0, 0.0)
    rank = dot(named.astype(BF16), before.astype(BF16))
    mine = (r // SLOTS) % 2 == block
    return jnp.where(mine & (named > 0.5) & (rank == (r % SLOTS).astype(F32)), 1.0, 0.0).astype(BF16)


def place_kernel(zh_ref, own_ref, other_ref, out_ref, both_ref):
    width = out_ref.shape[-1]
    zh = zh_ref[0]
    both_ref[0:8] = own_ref[:, :width]
    both_ref[8:16] = other_ref[:, :width]
    places = [placement(own_ref[:, width:], zh, 0), placement(other_ref[:, width:], zh, 1)]
    slots = dot(jnp.concatenate(places, axis=1), both_ref[...]).astype(BF16)
    for x in range(X):
        for y in range(Y):
            out_ref[x * Y + y] = slots[x * 2 * SLOTS : (x + 1) * 2 * SLOTS]


def placed(zh, own, other):
    width = own.shape[1] - META
    outs = [((X * Y, 2 * SLOTS, width), BF16)]
    return call(place_kernel, outs, (zh, own, other), "place", [pltpu.VMEM((16, width), BF16)])[0]


def ffn_kernel(a_ref, b_ref, wg_ref, wu_ref, wd_ref, pa_ref, pb_ref, rows_ref, hidden_ref):
    half, width = a_ref.shape
    rows_ref[:half] = a_ref[...]
    rows_ref[half:] = b_ref[...]
    block = 256
    for start in range(0, hidden_ref.shape[1], block):
        gate = dot(rows_ref[...], wg_ref[0, :, start : start + block])
        up = dot(rows_ref[...], wu_ref[0, :, start : start + block])
        hidden_ref[:, start : start + block] = (gate / (1.0 + jnp.exp(-gate)) * up).astype(BF16)
    for start in range(0, width, block):
        part = dot(hidden_ref[...], wd_ref[0, :, start : start + block])
        pa_ref[:, start : start + block] = part[:half]
        pb_ref[:, start : start + block] = part[half:].astype(BF16)


def ffn(a, b, wg, wu, wd):
    half, width = a.shape
    hidden = wg.shape[2]
    scratch = [pltpu.VMEM((2 * half, width), BF16), pltpu.VMEM((2 * half, hidden), BF16)]
    outs = [((half, width), F32), ((half, width), BF16)]
    return call(ffn_kernel, outs, (a, b, wg, wu, wd), "ffn", scratch, 16 * 2**20)


PIECES = 4


def load_kernel(*refs):
    sources, targets, sems = refs[1:4], refs[4:7], refs[7]
    copies = []
    for source, target in zip(sources, targets):
        rows = source.shape[1] // PIECES
        for piece in range(PIECES):
            part = pl.ds(piece * rows, rows)
            copies.append(pltpu.make_async_copy(source.at[0, part], target.at[0, part], sems.at[len(copies)]))
    for copy in copies:
        copy.start()
    for copy in copies:
        copy.wait()


def loaded(after, *weights):
    anywhere = pl.BlockSpec(memory_space=pl.ANY)
    return pl.pallas_call(
        load_kernel,
        out_shape=tuple(VMEM(w.shape, w.dtype) for w in weights),
        in_specs=[anywhere] * (1 + len(weights)),
        out_specs=tuple(pl.BlockSpec(memory_space=VMEM) for _ in weights),
        scratch_shapes=[pltpu.SemaphoreType.DMA((len(weights) * PIECES,))],
        cost_estimate=pl.CostEstimate(flops=0, transcendentals=0, bytes_accessed=2 * sum(w.size * 2 for w in weights)),
        compiler_params=pltpu.CompilerParams(vmem_limit_bytes=2**20),
        name="load",
    )(after, *in_hbm(*weights))


def mixing(meta, zh, block):
    rows = 8
    eye = jnp.where(iota((8, 8), 0) == iota((8, 8), 1), 1.0, 0.0).astype(BF16)
    fields = dot(eye, meta[:, :rows], ((1,), (1,)))
    lanes = X * Y * 2 * SLOTS
    r = iota((rows, lanes), 1)
    expert = ((r // (Y * 2 * SLOTS)) * ZH + zh).astype(F32)
    first = fields[:, 0:1] == expert
    second = fields[:, 1:2] == expert
    named = jnp.where(first | second, 1.0, 0.0)
    before = jnp.where(iota((rows, rows), 1) < iota((rows, rows), 0), 1.0, 0.0)
    rank = dot(before.astype(BF16), named.astype(BF16))
    w0 = fields[:, 2:3] + fields[:, 4:5] + fields[:, 6:7]
    w1 = fields[:, 3:4] + fields[:, 5:6] + fields[:, 7:8]
    mine = (r // SLOTS) % 2 == block
    weight = jnp.where(first, w0, jnp.where(second, w1, 0.0))
    return jnp.where(mine & (rank == (r % SLOTS).astype(F32)), weight, 0.0)


def mixed(weights, rows):
    high = weights.astype(BF16).astype(F32)
    mid = (weights - high).astype(BF16).astype(F32)
    parts = jnp.concatenate([high, mid, weights - high - mid], axis=0)
    total = dot(parts.astype(BF16), rows)
    return total[0:8] + total[8:16] + total[16:24]


def mix_kernel(zh_ref, rows_ref, packed_ref, out_ref, *, block):
    meta = packed_ref[:, rows_ref.shape[1] :]
    out_ref[...] = mixed(mixing(meta, zh_ref[0], block), rows_ref[...]).astype(out_ref.dtype)


def mix(zh, rows, source, block, dtype):
    kernel = functools.partial(mix_kernel, block=block)
    return call(kernel, [((8, rows.shape[1]), dtype)], (zh, rows, source), "mix%d" % block)[0]


def swapped(value, axis):
    return lax.ppermute(value, axis, [(0, 1), (1, 0)])


def on_device(tokens, expert_ids, gate_weights, gate_proj, up_proj, down_proj):
    width = tokens.shape[1]
    zh = lax.axis_index("zh").astype(jnp.int32).reshape(1)
    own = packed(tokens, expert_ids, gate_weights)
    other = swapped(own, "zh")
    weights = loaded(own, gate_proj, up_proj, down_proj)
    other, weights = lax.optimization_barrier((other, weights))
    slots = placed(zh, own, other)
    rows = lax.all_to_all(slots, ("x", "y"), 0, 0, tiled=True).reshape(-1, width)
    core_rows = swapped(rows, "core")
    part, core_part = ffn(rows, core_rows, *weights)
    pair = (part + swapped(core_part, "core").astype(F32)).astype(BF16)
    back = lax.all_to_all(pair.reshape(slots.shape), ("x", "y"), 0, 0, tiled=True)
    back = back.reshape(-1, width)
    arriving = swapped(mix(zh, back, other, 1, BF16), "zh")
    keep = mix(zh, back, own, 0, F32)
    return (keep + arriving.astype(F32)).astype(BF16)


def solution(mesh):
    dp = mesh.shape["dp"]
    fine = Mesh(mesh.devices.reshape(dp, X, ZH, Y, CORE), ("dp", "x", "zh", "y", "core"))
    every = P(("dp", "x", "zh", "y", "core"), None)
    return jax.shard_map(
        on_device,
        mesh=fine,
        in_specs=(
            every,
            every,
            every,
            P(("x", "zh"), None, ("y", "core")),
            P(("x", "zh"), None, ("y", "core")),
            P(("x", "zh"), ("y", "core"), None),
        ),
        out_specs=every,
        check_vma=False,
    )
```

time: 99.3 us -> 92.2 us (0.928)
  the two profiles are of different devices: /device:TPU:192 before, /device:TPU:32 now
where the time goes in v2:
time: 92.2 us; the launch traced here: 91.9 us
  blocking collectives  38.6 us (42%)
  starting transfers between devices  26 us (28%)
  Pallas kernels  13.9 us (15%)
  waiting for transfers between devices  12.5 us (14%)
    ppermute x4, starting transfers between devices, swapped(): return lax.ppermute(value, axis, [(0, 1), (1, 0)])  26 us
    all_to_all x1, blocking collectives, on_device(): lax.all_to_all(slots, ('x', 'y'), 0, 0, tiled=True).reshape(-1, width)  20.7 us
    all_to_all x1, blocking collectives, on_device(): lax.all_to_all(pair.reshape(slots.shape), ('x', 'y'), 0, 0, tiled=True)  17.9 us
    ppermute x4, waiting for transfers between devices, swapped(): return lax.ppermute(value, axis, [(0, 1), (1, 0)])  12.5 us
    pallas_call x4, Pallas kernels, call(): pl.pallas_call(kernel, out_shape=tuple((VMEM(shape, dtype) for shape, dty...  6.57 us
    pallas_call x1, Pallas kernels, loaded(): pl.pallas_call(load_kernel, out_shape=tuple((VMEM(w.shape, w.dtype) for w...  6.53 us
  transfers between devices with their start and end apart: 4, of which 3 were waited for; matrix products, arithmetic and copies ran while one was open for 0% of the time, Pallas kernels for 8%

profile of v2, /device:TPU:32, one launch (start us, length us, event | category | flops | bytes accessed | tf_op | source)
XLA Modules:
  0.0 91.9 jit_solution(4390007259263116564)
XLA Ops:
  0.0 0.8 pack.1.refs_0_.own_ref.packed_ref
  0.8 14.8 %collective-permute-start = (bf16[8,3200]{1,0:T(8,128)(2,1)S(1)}, bf16[8,3200]{1,0:T(8,128)(2,1)S(1)}, u32[]{:S(2)}, u32[]{:S(2)}) collective-permute-start(bf16[8,3200]{1,0:T(8,128)(2,1)S(1)} %pack.1.refs_0_.own_ref.packed_ref), channel_id=1, source_target_pairs={{0,8},{8,0},{1,9},{9,1},{2,10},{10,2},{3,11},{11,3},{4,12},{12,4},... | collective-permute-start | bytes 153608 | tf_op jit(solution)/shard_map/ppermute | solution.py:192
  15.7 6.5 %load.1 = (bf16[1,3072,1024]{2,1,0:T(8,128)(2,1)S(1)}, bf16[1,3072,1024]{2,1,0:T(8,128)(2,1)S(1)}, bf16[1,1024,3072]{2,1,0:T(8,128)(2,1)S(1)}) custom-call(bf16[8,3200]{1,0:T(8,128)(2,1)S(1)} %pack.1.refs_0_.own_ref.packed_ref, bf16[1,3072,1024]{2,1,0:T(8,128)(2,1)} %refs_1_.1, bf16[1,3072,1024]{2,1,0:T(8,128)(2,1)} %refs_2_.1, bf16[1,1024,3072]{2,1,0:T(8,128)(2,1)} %refs_3_.1), custom_call_target="tpu_custom_call" | custom-call | bytes 37748736 | tf_op jit(solution)/shard_map/load/pallas_call | solution.py:142
  22.2 0.0 collective-permute-done.other_ref.packed_ref
  22.2 0.4 place.1
  22.6 20.7 %all_to_all.10 = bf16[16,8,3072]{2,1,0:T(8,128)(2,1)S(1)} all-to-all(bf16[16,8,3072]{2,1,0:T(8,128)(2,1)S(1)} %place.1), channel_id=1, replica_groups=mesh['dp'=8,'x'=4,'zh'=2,'y'=4,'core'=2] {'x','y'}, dimensions={0} | all-to-all | bytes 1572864 | tf_op jit(solution)/shard_map/all_to_all | solution.py:203
  43.3 1.9 %collective-permute-start.1 = (bf16[128,3072]{1,0:T(8,128)(2,1)S(1)}, bf16[128,3072]{1,0:T(8,128)(2,1)S(1)}, u32[]{:S(2)}, u32[]{:S(2)}) collective-permute-start(bf16[128,3072]{1,0:T(8,128)(2,1)S(1)} %bitcast.9), channel_id=1, source_target_pairs={{0,1},{1,0},{2,3},{3,2},{4,5},{5,4},{6,7},{7,6},{8,9},{9,8},{10,11... | collective-permute-start | bytes 2359304 | tf_op jit(solution)/shard_map/ppermute | solution.py:192
  45.2 2.3 %collective-permute-done.1.b_ref = bf16[128,3072]{1,0:T(8,128)(2,1)S(1)} collective-permute-done((bf16[128,3072]{1,0:T(8,128)(2,1)S(1)}, bf16[128,3072]{1,0:T(8,128)(2,1)S(1)}, u32[]{:S(2)}, u32[]{:S(2)}) %collective-permute-start.1) | collective-permute-done | bytes 786464 | tf_op jit(solution)/shard_map/ppermute | solution.py:192
  47.4 5.2 %ffn.1 = (f32[128,3072]{1,0:T(8,128)S(1)}, bf16[128,3072]{1,0:T(8,128)(2,1)S(1)}) custom-call(bf16[128,3072]{1,0:T(8,128)(2,1)S(1)} %bitcast.10, bf16[128,3072]{1,0:T(8,128)(2,1)S(1)} %collective-permute-done.1.b_ref, bf16[1,3072,1024]{2,1,0:T(8,128)(2,1)S(1)} %get-tuple-element.18.wg_ref, bf16[1,3072,1024]{2,1,0:T(8,128)(2,1)S(1)} %get-tuple-element.19.wu_ref, ...), custom_call_target="tpu_custom_call" | custom-call | tf_op jit(solution)/shard_map/ffn/pallas_call | solution.py:29
  52.6 2.0 %collective-permute-start.2 = (bf16[128,3072]{1,0:T(8,128)(2,1)S(1)}, bf16[128,3072]{1,0:T(8,128)(2,1)S(1)}, u32[]{:S(2)}, u32[]{:S(2)}) collective-permute-start(bf16[128,3072]{1,0:T(8,128)(2,1)S(1)} %get-tuple-element.22), channel_id=1, source_target_pairs={{0,1},{1,0},{2,3},{3,2},{4,5},{5,4},{6,7},{7,6},{8,9},{9,8},{10,11... | collective-permute-start | bytes 2359304 | tf_op jit(solution)/shard_map/ppermute | solution.py:192
  54.7 2.1 %collective-permute-done.2 = bf16[128,3072]{1,0:T(8,128)(2,1)S(1)} collective-permute-done((bf16[128,3072]{1,0:T(8,128)(2,1)S(1)}, bf16[128,3072]{1,0:T(8,128)(2,1)S(1)}, u32[]{:S(2)}, u32[]{:S(2)}) %collective-permute-start.2) | collective-permute-done | bytes 786464 | tf_op jit(solution)/shard_map/ppermute | solution.py:192
  56.8 0.2 fusion
  57.0 17.9 %all_to_all.11 = bf16[16,8,3072]{2,1,0:T(8,128)(2,1)S(1)} all-to-all(bf16[16,8,3072]{2,1,0:T(8,128)(2,1)S(1)} %fusion), channel_id=1, replica_groups=mesh['dp'=8,'x'=4,'zh'=2,'y'=4,'core'=2] {'x','y'}, dimensions={0} | all-to-all | bytes 1572864 | tf_op jit(solution)/shard_map/all_to_all | solution.py:207
  74.9 0.5 mix1.1
  75.4 7.2 %collective-permute-start.3 = (bf16[8,3072]{1,0:T(8,128)(2,1)S(1)}, bf16[8,3072]{1,0:T(8,128)(2,1)S(1)}, u32[]{:S(2)}, u32[]{:S(2)}) collective-permute-start(bf16[8,3072]{1,0:T(8,128)(2,1)S(1)} %mix1.1), channel_id=1, source_target_pairs={{0,8},{8,0},{1,9},{9,1},{2,10},{10,2},{3,11},{11,3},{4,12},{12,4},... | collective-permute-start | bytes 147464 | tf_op jit(solution)/shard_map/ppermute | solution.py:192
  82.7 0.5 mix0.1
  83.2 8.1 %collective-permute-done.3 = bf16[8,3072]{1,0:T(8,128)(2,1)S(1)} collective-permute-done((bf16[8,3072]{1,0:T(8,128)(2,1)S(1)}, bf16[8,3072]{1,0:T(8,128)(2,1)S(1)}, u32[]{:S(2)}, u32[]{:S(2)}) %collective-permute-start.3) | collective-permute-done | bytes 49184 | tf_op jit(solution)/shard_map/ppermute | solution.py:192
  91.3 0.6 add_convert_fusion.1
Async XLA Ops:
  0.8 21.4 %collective-permute-start = (bf16[8,3200]{1,0:T(8,128)(2,1)S(1)}, bf16[8,3200]{1,0:T(8,128)(2,1)S(1)}, u32[]{:S(2)}, u32[]{:S(2)}) collective-permute-start(bf16[8,3200]{1,0:T(8,128)(2,1)S(1)} %pack.1.refs_0_.own_ref.packed_ref), channel_id=1, source_target_pairs={{0,8},{8,0},{1,9},{9,1},{2,10},{10,2},{3,11},{11,3},{4,12},{12,4},... | collective-permute-start | bytes 153608 | tf_op jit(solution)/shard_map/ppermute | solution.py:192
  43.3 4.2 %collective-permute-start.1 = (bf16[128,3072]{1,0:T(8,128)(2,1)S(1)}, bf16[128,3072]{1,0:T(8,128)(2,1)S(1)}, u32[]{:S(2)}, u32[]{:S(2)}) collective-permute-start(bf16[128,3072]{1,0:T(8,128)(2,1)S(1)} %bitcast.9), channel_id=1, source_target_pairs={{0,1},{1,0},{2,3},{3,2},{4,5},{5,4},{6,7},{7,6},{8,9},{9,8},{10,11... | collective-permute-start | bytes 2359304 | tf_op jit(solution)/shard_map/ppermute | solution.py:192
  52.6 4.2 %collective-permute-start.2 = (bf16[128,3072]{1,0:T(8,128)(2,1)S(1)}, bf16[128,3072]{1,0:T(8,128)(2,1)S(1)}, u32[]{:S(2)}, u32[]{:S(2)}) collective-permute-start(bf16[128,3072]{1,0:T(8,128)(2,1)S(1)} %get-tuple-element.22), channel_id=1, source_target_pairs={{0,1},{1,0},{2,3},{3,2},{4,5},{5,4},{6,7},{7,6},{8,9},{9,8},{10,11... | collective-permute-start | bytes 2359304 | tf_op jit(solution)/shard_map/ppermute | solution.py:192
  75.4 15.9 %collective-permute-start.3 = (bf16[8,3072]{1,0:T(8,128)(2,1)S(1)}, bf16[8,3072]{1,0:T(8,128)(2,1)S(1)}, u32[]{:S(2)}, u32[]{:S(2)}) collective-permute-start(bf16[8,3072]{1,0:T(8,128)(2,1)S(1)} %mix1.1), channel_id=1, source_target_pairs={{0,8},{8,0},{1,9},{9,1},{2,10},{10,2},{3,11},{11,3},{4,12},{12,4},... | collective-permute-start | bytes 147464 | tf_op jit(solution)/shard_map/ppermute | solution.py:192

commit v3 on v2

--- a/solution.py
+++ b/solution.py
@@ -23,7 +23,7 @@
     return lax.broadcasted_iota(jnp.int32, shape, dim)
 
 
-def call(kernel, outs, args, name, scratch=(), limit=4 * 2**20):
+def call(kernel, outs, args, name, scratch=(), limit=8 * 2**20, flops=0):
     specs = [pl.BlockSpec(memory_space=SMEM if a.size == 1 else VMEM) for a in args]
     args = [a if a.size == 1 else pltpu.with_memory_space_constraint(a, VMEM) for a in args]
     return pl.pallas_call(
@@ -33,6 +33,7 @@
         out_specs=tuple(pl.BlockSpec(memory_space=VMEM) for _ in outs),
         scratch_shapes=scratch,
         compiler_params=pltpu.CompilerParams(vmem_limit_bytes=limit),
+        cost_estimate=pl.CostEstimate(flops=flops, transcendentals=0, bytes_accessed=0) if flops else None,
         name=name,
     )(*args)
 
@@ -97,27 +98,32 @@
     return call(place_kernel, outs, (zh, own, other), "place", [pltpu.VMEM((16, width), BF16)])[0]
 
 
-def ffn_kernel(a_ref, b_ref, wg_ref, wu_ref, wd_ref, pa_ref, pb_ref, rows_ref, hidden_ref):
-    half, width = a_ref.shape
-    rows_ref[:half] = a_ref[...]
-    rows_ref[half:] = b_ref[...]
-    block = 256
-    for start in range(0, hidden_ref.shape[1], block):
-        gate = dot(rows_ref[...], wg_ref[0, :, start : start + block])
-        up = dot(rows_ref[...], wu_ref[0, :, start : start + block])
-        hidden_ref[:, start : start + block] = (gate / (1.0 + jnp.exp(-gate)) * up).astype(BF16)
-    for start in range(0, width, block):
-        part = dot(hidden_ref[...], wd_ref[0, :, start : start + block])
-        pa_ref[:, start : start + block] = part[:half]
-        pb_ref[:, start : start + block] = part[half:].astype(BF16)
-
-
-def ffn(a, b, wg, wu, wd):
-    half, width = a.shape
-    hidden = wg.shape[2]
-    scratch = [pltpu.VMEM((2 * half, width), BF16), pltpu.VMEM((2 * half, hidden), BF16)]
-    outs = [((half, width), F32), ((half, width), BF16)]
-    return call(ffn_kernel, outs, (a, b, wg, wu, wd), "ffn", scratch, 16 * 2**20)
+BLOCK = 256
+
+
+def hidden_units(rows, wg_ref, wu_ref, out_ref):
+    for start in range(0, out_ref.shape[1], BLOCK):
+        gate = dot(rows, wg_ref[0, :, start : start + BLOCK])
+        up = dot(rows, wu_ref[0, :, start : start + BLOCK])
+        out_ref[:, start : start + BLOCK] = (gate / (1.0 + jnp.exp(-gate)) * up).astype(BF16)
+
+
+def down(hidden, wd_ref, out_ref):
+    for start in range(0, out_ref.shape[1], BLOCK):
+        out_ref[:, start : start + BLOCK] = dot(hidden, wd_ref[0, :, start : start + BLOCK]).astype(out_ref.dtype)
+
+
+def hidden_kernel(rows_ref, wg_ref, wu_ref, out_ref):
+    hidden_units(rows_ref[...], wg_ref, wu_ref, out_ref)
+
+
+def down_kernel(hidden_ref, wd_ref, out_ref):
+    down(hidden_ref[...], wd_ref, out_ref)
+
+
+def expert_kernel(rows_ref, wg_ref, wu_ref, wd_ref, out_ref, hidden_ref):
+    hidden_units(rows_ref[...], wg_ref, wu_ref, hidden_ref)
+    down(hidden_ref[...], wd_ref, out_ref)
 
 
 PIECES = 4
@@ -170,22 +176,25 @@
     return jnp.where(mine & (rank == (r % SLOTS).astype(F32)), weight, 0.0)
 
 
-def mixed(weights, rows):
+def split(weights):
     high = weights.astype(BF16).astype(F32)
     mid = (weights - high).astype(BF16).astype(F32)
-    parts = jnp.concatenate([high, mid, weights - high - mid], axis=0)
-    total = dot(parts.astype(BF16), rows)
-    return total[0:8] + total[8:16] + total[16:24]
-
-
-def mix_kernel(zh_ref, rows_ref, packed_ref, out_ref, *, block):
-    meta = packed_ref[:, rows_ref.shape[1] :]
-    out_ref[...] = mixed(mixing(meta, zh_ref[0], block), rows_ref[...]).astype(out_ref.dtype)
-
-
-def mix(zh, rows, source, block, dtype):
-    kernel = functools.partial(mix_kernel, block=block)
-    return call(kernel, [((8, rows.shape[1]), dtype)], (zh, rows, source), "mix%d" % block)[0]
+    return jnp.concatenate([high, mid, weights - high - mid], axis=0).astype(BF16)
+
+
+def weights_kernel(zh_ref, own_ref, other_ref, after_ref, own_out, other_out):
+    width = own_ref.shape[1] - META
+    own_out[...] = split(mixing(own_ref[:, width:], zh_ref[0], 0))
+    other_out[...] = split(mixing(other_ref[:, width:], zh_ref[0], 1))
+
+
+def mix_kernel(weights_ref, rows_ref, out_ref):
+    total = dot(weights_ref[...], rows_ref[...])
+    out_ref[...] = (total[0:8] + total[8:16] + total[16:24]).astype(out_ref.dtype)
+
+
+def mix(weights, rows, dtype, name):
+    return call(mix_kernel, [((8, rows.shape[1]), dtype)], (weights, rows), name, flops=2 * weights.shape[0] * rows.size)[0]
 
 
 def swapped(value, axis):
@@ -194,20 +203,30 @@
 
 def on_device(tokens, expert_ids, gate_weights, gate_proj, up_proj, down_proj):
     width = tokens.shape[1]
+    units = gate_proj.shape[2]
     zh = lax.axis_index("zh").astype(jnp.int32).reshape(1)
     own = packed(tokens, expert_ids, gate_weights)
     other = swapped(own, "zh")
     weights = loaded(own, gate_proj, up_proj, down_proj)
-    other, weights = lax.optimization_barrier((other, weights))
+    other, (wg, wu, wd) = lax.optimization_barrier((other, weights))
     slots = placed(zh, own, other)
-    rows = lax.all_to_all(slots, ("x", "y"), 0, 0, tiled=True).reshape(-1, width)
+    half = slots.shape[0] * slots.shape[1]
+    rows = lax.all_to_all(slots, ("x", "y"), 0, 0, tiled=True).reshape(half, width)
     core_rows = swapped(rows, "core")
-    part, core_part = ffn(rows, core_rows, *weights)
-    pair = (part + swapped(core_part, "core").astype(F32)).astype(BF16)
-    back = lax.all_to_all(pair.reshape(slots.shape), ("x", "y"), 0, 0, tiled=True)
-    back = back.reshape(-1, width)
-    arriving = swapped(mix(zh, back, other, 1, BF16), "zh")
-    keep = mix(zh, back, own, 0, F32)
+    third = 2 * half * width * units
+    hidden = call(hidden_kernel, [((half, units), BF16)], (rows, wg, wu), "hidden", flops=2 * third)[0]
+    core_rows, hidden = lax.optimization_barrier((core_rows, hidden))
+    scratch = [pltpu.VMEM((half, units), BF16)]
+    core_part = call(expert_kernel, [((half, width), BF16)], (core_rows, wg, wu, wd), "expert", scratch, flops=3 * third)[0]
+    arrived = swapped(core_part, "core")
+    part = call(down_kernel, [((half, width), F32)], (hidden, wd), "down", flops=third)[0]
+    pair = (part + arrived.astype(F32)).astype(BF16).reshape(slots.shape)
+    back = lax.all_to_all(pair, ("x", "y"), 0, 0, tiled=True)
+    outs = [((24, half), BF16), ((24, half), BF16)]
+    own_weights, other_weights = call(weights_kernel, outs, (zh, own, other, pair), "weights", flops=2**28)
+    back = back.reshape(half, width)
+    arriving = swapped(mix(other_weights, back, BF16, "mix_other"), "zh")
+    keep = mix(own_weights, back, F32, "mix_own")
     return (keep + arriving.astype(F32)).astype(BF16)
 
 

time: 92.2 us -> 90.4 us (0.980)
  the two profiles are of different devices: /device:TPU:32 before, /device:TPU:64 now
where the time goes in v3:
time: 90.4 us; the launch traced here: 90 us
  starting transfers between devices  30.2 us (33%)
  waiting for transfers between devices  21.8 us (24%)
  blocking collectives  20.7 us (23%)
  Pallas kernels  15.6 us (17%)
  other arithmetic  1.68 us (2%)
    ppermute x4, starting transfers between devices, swapped(): return lax.ppermute(value, axis, [(0, 1), (1, 0)])  26.5 us
    all_to_all x1, blocking collectives, on_device(): lax.all_to_all(slots, ('x', 'y'), 0, 0, tiled=True).reshape(half, width)  20.7 us
    all_to_all x1, waiting for transfers between devices, on_device(): back = lax.all_to_all(pair, ('x', 'y'), 0, 0, tiled=True)  13.5 us
    ppermute x4, waiting for transfers between devices, swapped(): return lax.ppermute(value, axis, [(0, 1), (1, 0)])  8.29 us
    pallas_call x7, Pallas kernels, call(): pl.pallas_call(kernel, out_shape=tuple((VMEM(shape, dtype) for shape, dty...  8.23 us
    pallas_call x1, Pallas kernels, loaded(): pl.pallas_call(load_kernel, out_shape=tuple((VMEM(w.shape, w.dtype) for w...  6.53 us
    all_to_all x1, starting transfers between devices, on_device(): back = lax.all_to_all(pair, ('x', 'y'), 0, 0, tiled=True)  3.67 us
  transfers between devices with their start and end apart: 5, of which 4 were waited for; matrix products, arithmetic and copies ran while one was open for 0% of the time, Pallas kernels for 13%

profile of v3, /device:TPU:64, one launch (start us, length us, event | category | flops | bytes accessed | tf_op | source)
XLA Modules:
  0.0 90.0 jit_solution(11811406705322480181)
XLA Ops:
  0.0 0.8 pack.1.refs_0_.own_ref
  0.8 13.9 %collective-permute-start = (bf16[8,3200]{1,0:T(8,128)(2,1)S(1)}, bf16[8,3200]{1,0:T(8,128)(2,1)S(1)}, u32[]{:S(2)}, u32[]{:S(2)}) collective-permute-start(bf16[8,3200]{1,0:T(8,128)(2,1)S(1)} %pack.1.refs_0_.own_ref), channel_id=1, source_target_pairs={{0,8},{8,0},{1,9},{9,1},{2,10},{10,2},{3,11},{11,3},{4,12},{12,4},... | collective-permute-start | bytes 153608 | tf_op jit(solution)/shard_map/ppermute | solution.py:201
  14.8 6.5 %load.1 = (bf16[1,3072,1024]{2,1,0:T(8,128)(2,1)S(1)}, bf16[1,3072,1024]{2,1,0:T(8,128)(2,1)S(1)}, bf16[1,1024,3072]{2,1,0:T(8,128)(2,1)S(1)}) custom-call(bf16[8,3200]{1,0:T(8,128)(2,1)S(1)} %pack.1.refs_0_.own_ref, bf16[1,3072,1024]{2,1,0:T(8,128)(2,1)} %refs_1_.1, bf16[1,3072,1024]{2,1,0:T(8,128)(2,1)} %refs_2_.1, bf16[1,1024,3072]{2,1,0:T(8,128)(2,1)} %refs_3_.1), custom_call_target="tpu_custom_call" | custom-call | bytes 37748736 | tf_op jit(solution)/shard_map/load/pallas_call | solution.py:148
  21.3 0.0 collective-permute-done.other_ref
  21.3 0.4 place.1
  21.7 20.7 %all_to_all.10 = bf16[16,8,3072]{2,1,0:T(8,128)(2,1)S(1)} all-to-all(bf16[16,8,3072]{2,1,0:T(8,128)(2,1)S(1)} %place.1), channel_id=1, replica_groups=mesh['dp'=8,'x'=4,'zh'=2,'y'=4,'core'=2] {'x','y'}, dimensions={0} | all-to-all | bytes 1572864 | tf_op jit(solution)/shard_map/all_to_all | solution.py:214
  42.4 1.9 %collective-permute-start.1 = (bf16[128,3072]{1,0:T(8,128)(2,1)S(1)}, bf16[128,3072]{1,0:T(8,128)(2,1)S(1)}, u32[]{:S(2)}, u32[]{:S(2)}) collective-permute-start(bf16[128,3072]{1,0:T(8,128)(2,1)S(1)} %bitcast.9), channel_id=1, source_target_pairs={{0,1},{1,0},{2,3},{3,2},{4,5},{5,4},{6,7},{7,6},{8,9},{9,8},{10,11... | collective-permute-start | bytes 2359304 | tf_op jit(solution)/shard_map/ppermute | solution.py:201
  44.3 1.9 %hidden.1.hidden_ref = bf16[128,1024]{1,0:T(8,128)(2,1)S(1)} custom-call(bf16[128,3072]{1,0:T(8,128)(2,1)S(1)} %bitcast.10, bf16[1,3072,1024]{2,1,0:T(8,128)(2,1)S(1)} %get-tuple-element.20.wg_ref, bf16[1,3072,1024]{2,1,0:T(8,128)(2,1)S(1)} %get-tuple-element.21.wu_ref), custom_call_target="tpu_custom_call" | custom-call | flops 1610612736 | tf_op jit(solution)/shard_map/hidden/pallas_call | solution.py:29
  46.3 0.3 collective-permute-done.1.rows_ref
  46.5 2.8 %expert.1 = bf16[128,3072]{1,0:T(8,128)(2,1)S(1)} custom-call(bf16[128,3072]{1,0:T(8,128)(2,1)S(1)} %collective-permute-done.1.rows_ref, bf16[1,3072,1024]{2,1,0:T(8,128)(2,1)S(1)} %get-tuple-element.20.wg_ref, bf16[1,3072,1024]{2,1,0:T(8,128)(2,1)S(1)} %get-tuple-element.21.wu_ref, bf16[1,1024,3072]{2,1,0:T(8,128)(2,1)S(1)} %get-tuple-element.23.wd_ref), custom_call_target="tpu_custom_call" | custom-call | flops 2415919104 | tf_op jit(solution)/shard_map/expert/pallas_call | solution.py:29
  49.3 2.1 %collective-permute-start.2 = (bf16[128,3072]{1,0:T(8,128)(2,1)S(1)}, bf16[128,3072]{1,0:T(8,128)(2,1)S(1)}, u32[]{:S(2)}, u32[]{:S(2)}) collective-permute-start(bf16[128,3072]{1,0:T(8,128)(2,1)S(1)} %expert.1), channel_id=1, source_target_pairs={{0,1},{1,0},{2,3},{3,2},{4,5},{5,4},{6,7},{7,6},{8,9},{9,8},{10,11... | collective-permute-start | bytes 2359304 | tf_op jit(solution)/shard_map/ppermute | solution.py:201
  51.5 1.0 %down.1 = f32[128,3072]{1,0:T(8,128)S(1)} custom-call(bf16[128,1024]{1,0:T(8,128)(2,1)S(1)} %hidden.1.hidden_ref, bf16[1,1024,3072]{2,1,0:T(8,128)(2,1)S(1)} %get-tuple-element.23.wd_ref), custom_call_target="tpu_custom_call" | custom-call | flops 805306368 | tf_op jit(solution)/shard_map/down/pallas_call | solution.py:29
  52.5 1.0 %collective-permute-done.2 = bf16[128,3072]{1,0:T(8,128)(2,1)S(1)} collective-permute-done((bf16[128,3072]{1,0:T(8,128)(2,1)S(1)}, bf16[128,3072]{1,0:T(8,128)(2,1)S(1)}, u32[]{:S(2)}, u32[]{:S(2)}) %collective-permute-start.2) | collective-permute-done | bytes 786464 | tf_op jit(solution)/shard_map/ppermute | solution.py:201
  53.5 1.0 %fusion.after_ref = bf16[16,8,3072]{2,1,0:T(8,128)(2,1)} fusion(f32[128,3072]{1,0:T(8,128)S(1)} %down.1, bf16[128,3072]{1,0:T(8,128)(2,1)S(1)} %collective-permute-done.2), kind=kLoop, calls=%fused_computation.1 | loop fusion | flops 1179648 | bytes 3145728 | tf_op jit(solution)/shard_map/reshape | solution.py:223
  54.6 3.7 %all-to-all-start.1 = ((bf16[16,8,3072]{2,1,0:T(8,128)(2,1)}), bf16[16,8,3072]{2,1,0:T(8,128)(2,1)S(1)}, u32[]{:S(2)}, u32[]{:S(2)}) async-start(bf16[16,8,3072]{2,1,0:T(8,128)(2,1)} %fusion.after_ref), calls=%async_computation.1 | async-start | bytes 1572864 | tf_op jit(solution)/shard_map/all_to_all | solution.py:224
  58.2 1.7 %weights.1 = (bf16[24,128]{1,0:T(8,128)(2,1)S(1)}, bf16[24,128]{1,0:T(8,128)(2,1)S(1)}) custom-call(s32[1]{0:T(128)} %bitcast.zh_ref, bf16[8,3200]{1,0:T(8,128)(2,1)S(1)} %pack.1.refs_0_.own_ref, bf16[8,3200]{1,0:T(8,128)(2,1)S(1)} %collective-permute-done.other_ref, bf16[16,8,3072]{2,1,0:T(8,128)(2,1)} %fusion.after_ref), custom_call_target="tpu_custom_call" | custom-call | flops 268435456 | tf_op jit(solution)/shard_map/weights/pallas_call | solution.py:29
  59.9 13.5 %all-to-all-done.1 = bf16[16,8,3072]{2,1,0:T(8,128)(2,1)S(1)} async-done(((bf16[16,8,3072]{2,1,0:T(8,128)(2,1)}), bf16[16,8,3072]{2,1,0:T(8,128)(2,1)S(1)}, u32[]{:S(2)}, u32[]{:S(2)}) %all-to-all-start.1) | async-done | bytes 786464 | tf_op jit(solution)/shard_map/all_to_all | solution.py:224
  73.4 0.2 mix_other.1
  73.6 8.6 %collective-permute-start.3 = (bf16[8,3072]{1,0:T(8,128)(2,1)S(1)}, bf16[8,3072]{1,0:T(8,128)(2,1)S(1)}, u32[]{:S(2)}, u32[]{:S(2)}) collective-permute-start(bf16[8,3072]{1,0:T(8,128)(2,1)S(1)} %mix_other.1), channel_id=1, source_target_pairs={{0,8},{8,0},{1,9},{9,1},{2,10},{10,2},{3,11},{11,3},{4,12},{12,4},... | collective-permute-start | bytes 147464 | tf_op jit(solution)/shard_map/ppermute | solution.py:201
  82.2 0.2 mix_own.1
  82.4 7.0 %collective-permute-done.3 = bf16[8,3072]{1,0:T(8,128)(2,1)S(1)} collective-permute-done((bf16[8,3072]{1,0:T(8,128)(2,1)S(1)}, bf16[8,3072]{1,0:T(8,128)(2,1)S(1)}, u32[]{:S(2)}, u32[]{:S(2)}) %collective-permute-start.3) | collective-permute-done | bytes 49184 | tf_op jit(solution)/shard_map/ppermute | solution.py:201
  89.4 0.6 add_convert_fusion.1
Async XLA Ops:
  0.8 20.5 %collective-permute-start = (bf16[8,3200]{1,0:T(8,128)(2,1)S(1)}, bf16[8,3200]{1,0:T(8,128)(2,1)S(1)}, u32[]{:S(2)}, u32[]{:S(2)}) collective-permute-start(bf16[8,3200]{1,0:T(8,128)(2,1)S(1)} %pack.1.refs_0_.own_ref), channel_id=1, source_target_pairs={{0,8},{8,0},{1,9},{9,1},{2,10},{10,2},{3,11},{11,3},{4,12},{12,4},... | collective-permute-start | bytes 153608 | tf_op jit(solution)/shard_map/ppermute | solution.py:201
  42.4 4.2 %collective-permute-start.1 = (bf16[128,3072]{1,0:T(8,128)(2,1)S(1)}, bf16[128,3072]{1,0:T(8,128)(2,1)S(1)}, u32[]{:S(2)}, u32[]{:S(2)}) collective-permute-start(bf16[128,3072]{1,0:T(8,128)(2,1)S(1)} %bitcast.9), channel_id=1, source_target_pairs={{0,1},{1,0},{2,3},{3,2},{4,5},{5,4},{6,7},{7,6},{8,9},{9,8},{10,11... | collective-permute-start | bytes 2359304 | tf_op jit(solution)/shard_map/ppermute | solution.py:201
  49.3 4.2 %collective-permute-start.2 = (bf16[128,3072]{1,0:T(8,128)(2,1)S(1)}, bf16[128,3072]{1,0:T(8,128)(2,1)S(1)}, u32[]{:S(2)}, u32[]{:S(2)}) collective-permute-start(bf16[128,3072]{1,0:T(8,128)(2,1)S(1)} %expert.1), channel_id=1, source_target_pairs={{0,1},{1,0},{2,3},{3,2},{4,5},{5,4},{6,7},{7,6},{8,9},{9,8},{10,11... | collective-permute-start | bytes 2359304 | tf_op jit(solution)/shard_map/ppermute | solution.py:201
  54.6 18.8 %all-to-all-start.1 = ((bf16[16,8,3072]{2,1,0:T(8,128)(2,1)}), bf16[16,8,3072]{2,1,0:T(8,128)(2,1)S(1)}, u32[]{:S(2)}, u32[]{:S(2)}) async-start(bf16[16,8,3072]{2,1,0:T(8,128)(2,1)} %fusion.after_ref), calls=%async_computation.1 | async-start | bytes 1572864 | tf_op jit(solution)/shard_map/all_to_all | solution.py:224
  73.6 15.8 %collective-permute-start.3 = (bf16[8,3072]{1,0:T(8,128)(2,1)S(1)}, bf16[8,3072]{1,0:T(8,128)(2,1)S(1)}, u32[]{:S(2)}, u32[]{:S(2)}) collective-permute-start(bf16[8,3072]{1,0:T(8,128)(2,1)S(1)} %mix_other.1), channel_id=1, source_target_pairs={{0,8},{8,0},{1,9},{9,1},{2,10},{10,2},{3,11},{11,3},{4,12},{12,4},... | collective-permute-start | bytes 147464 | tf_op jit(solution)/shard_map/ppermute | solution.py:201

commit v4 on v3

--- a/solution.py
+++ b/solution.py
@@ -182,7 +182,7 @@
     return jnp.concatenate([high, mid, weights - high - mid], axis=0).astype(BF16)
 
 
-def weights_kernel(zh_ref, own_ref, other_ref, after_ref, own_out, other_out):
+def weights_kernel(zh_ref, own_ref, other_ref, own_out, other_out):
     width = own_ref.shape[1] - META
     own_out[...] = split(mixing(own_ref[:, width:], zh_ref[0], 0))
     other_out[...] = split(mixing(other_ref[:, width:], zh_ref[0], 1))
@@ -218,12 +218,14 @@
     core_rows, hidden = lax.optimization_barrier((core_rows, hidden))
     scratch = [pltpu.VMEM((half, units), BF16)]
     core_part = call(expert_kernel, [((half, width), BF16)], (core_rows, wg, wu, wd), "expert", scratch, flops=3 * third)[0]
+    core_part, own, other = lax.optimization_barrier((core_part, own, other))
     arrived = swapped(core_part, "core")
     part = call(down_kernel, [((half, width), F32)], (hidden, wd), "down", flops=third)[0]
+    outs = [((24, half), BF16), ((24, half), BF16)]
+    mixers = call(weights_kernel, outs, (zh, own, other), "weights", flops=2**28)
+    arrived, part, (own_weights, other_weights) = lax.optimization_barrier((arrived, part, mixers))
     pair = (part + arrived.astype(F32)).astype(BF16).reshape(slots.shape)
     back = lax.all_to_all(pair, ("x", "y"), 0, 0, tiled=True)
-    outs = [((24, half), BF16), ((24, half), BF16)]
-    own_weights, other_weights = call(weights_kernel, outs, (zh, own, other, pair), "weights", flops=2**28)
     back = back.reshape(half, width)
     arriving = swapped(mix(other_weights, back, BF16, "mix_other"), "zh")
     keep = mix(own_weights, back, F32, "mix_own")

time: 90.4 us -> 89.6 us (level)
  the two profiles are of different devices: /device:TPU:64 before, /device:TPU:32 now
where the time goes in v4:
time: 89.6 us; the launch traced here: 89.3 us
  blocking collectives  38.7 us (43%)
  starting transfers between devices  26.1 us (29%)
  Pallas kernels  14.4 us (16%)
  waiting for transfers between devices  9.24 us (10%)
    ppermute x4, starting transfers between devices, swapped(): return lax.ppermute(value, axis, [(0, 1), (1, 0)])  26.1 us
    all_to_all x1, blocking collectives, on_device(): lax.all_to_all(slots, ('x', 'y'), 0, 0, tiled=True).reshape(half, width)  20.7 us
    all_to_all x1, blocking collectives, on_device(): back = lax.all_to_all(pair, ('x', 'y'), 0, 0, tiled=True)  18 us
    ppermute x4, waiting for transfers between devices, swapped(): return lax.ppermute(value, axis, [(0, 1), (1, 0)])  9.24 us
    pallas_call x7, Pallas kernels, call(): pl.pallas_call(kernel, out_shape=tuple((VMEM(shape, dtype) for shape, dty...  7.06 us
    pallas_call x1, Pallas kernels, loaded(): pl.pallas_call(load_kernel, out_shape=tuple((VMEM(w.shape, w.dtype) for w...  6.53 us
  transfers between devices with their start and end apart: 4, of which 3 were waited for; matrix products, arithmetic and copies ran while one was open for 0% of the time, Pallas kernels for 11%

profile of v4, /device:TPU:32, one launch (start us, length us, event | category | flops | bytes accessed | tf_op | source)
XLA Modules:
  0.0 89.3 jit_solution(1875725121949567991)
XLA Ops:
  0.0 0.8 pack.1.refs_0_.own_ref
  0.8 14.8 %collective-permute-start = (bf16[8,3200]{1,0:T(8,128)(2,1)S(1)}, bf16[8,3200]{1,0:T(8,128)(2,1)S(1)}, u32[]{:S(2)}, u32[]{:S(2)}) collective-permute-start(bf16[8,3200]{1,0:T(8,128)(2,1)S(1)} %pack.1.refs_0_.own_ref), channel_id=1, source_target_pairs={{0,8},{8,0},{1,9},{9,1},{2,10},{10,2},{3,11},{11,3},{4,12},{12,4},... | collective-permute-start | bytes 153608 | tf_op jit(solution)/shard_map/ppermute | solution.py:201
  15.7 6.5 %load.1 = (bf16[1,3072,1024]{2,1,0:T(8,128)(2,1)S(1)}, bf16[1,3072,1024]{2,1,0:T(8,128)(2,1)S(1)}, bf16[1,1024,3072]{2,1,0:T(8,128)(2,1)S(1)}) custom-call(bf16[8,3200]{1,0:T(8,128)(2,1)S(1)} %pack.1.refs_0_.own_ref, bf16[1,3072,1024]{2,1,0:T(8,128)(2,1)} %refs_1_.1, bf16[1,3072,1024]{2,1,0:T(8,128)(2,1)} %refs_2_.1, bf16[1,1024,3072]{2,1,0:T(8,128)(2,1)} %refs_3_.1), custom_call_target="tpu_custom_call" | custom-call | bytes 37748736 | tf_op jit(solution)/shard_map/load/pallas_call | solution.py:148
  22.2 0.0 collective-permute-done.other_ref
  22.2 0.4 place.1
  22.6 20.7 %all_to_all.10 = bf16[16,8,3072]{2,1,0:T(8,128)(2,1)S(1)} all-to-all(bf16[16,8,3072]{2,1,0:T(8,128)(2,1)S(1)} %place.1), channel_id=1, replica_groups=mesh['dp'=8,'x'=4,'zh'=2,'y'=4,'core'=2] {'x','y'}, dimensions={0} | all-to-all | bytes 1572864 | tf_op jit(solution)/shard_map/all_to_all | solution.py:214
  43.3 1.9 %collective-permute-start.1 = (bf16[128,3072]{1,0:T(8,128)(2,1)S(1)}, bf16[128,3072]{1,0:T(8,128)(2,1)S(1)}, u32[]{:S(2)}, u32[]{:S(2)}) collective-permute-start(bf16[128,3072]{1,0:T(8,128)(2,1)S(1)} %bitcast.9), channel_id=1, source_target_pairs={{0,1},{1,0},{2,3},{3,2},{4,5},{5,4},{6,7},{7,6},{8,9},{9,8},{10,11... | collective-permute-start | bytes 2359304 | tf_op jit(solution)/shard_map/ppermute | solution.py:201
  45.2 1.9 %hidden.1.hidden_ref = bf16[128,1024]{1,0:T(8,128)(2,1)S(1)} custom-call(bf16[128,3072]{1,0:T(8,128)(2,1)S(1)} %bitcast.10, bf16[1,3072,1024]{2,1,0:T(8,128)(2,1)S(1)} %get-tuple-element.27.wg_ref, bf16[1,3072,1024]{2,1,0:T(8,128)(2,1)S(1)} %get-tuple-element.28.wu_ref), custom_call_target="tpu_custom_call" | custom-call | flops 1610612736 | tf_op jit(solution)/shard_map/hidden/pallas_call | solution.py:29
  47.1 0.3 collective-permute-done.1.rows_ref
  47.4 2.8 %expert.1 = bf16[128,3072]{1,0:T(8,128)(2,1)S(1)} custom-call(bf16[128,3072]{1,0:T(8,128)(2,1)S(1)} %collective-permute-done.1.rows_ref, bf16[1,3072,1024]{2,1,0:T(8,128)(2,1)S(1)} %get-tuple-element.27.wg_ref, bf16[1,3072,1024]{2,1,0:T(8,128)(2,1)S(1)} %get-tuple-element.28.wu_ref, bf16[1,1024,3072]{2,1,0:T(8,128)(2,1)S(1)} %get-tuple-element.30.wd_ref), custom_call_target="tpu_custom_call" | custom-call | flops 2415919104 | tf_op jit(solution)/shard_map/expert/pallas_call | solution.py:29
  50.2 2.1 %collective-permute-start.2 = (bf16[128,3072]{1,0:T(8,128)(2,1)S(1)}, bf16[128,3072]{1,0:T(8,128)(2,1)S(1)}, u32[]{:S(2)}, u32[]{:S(2)}) collective-permute-start(bf16[128,3072]{1,0:T(8,128)(2,1)S(1)} %expert.1), channel_id=1, source_target_pairs={{0,1},{1,0},{2,3},{3,2},{4,5},{5,4},{6,7},{7,6},{8,9},{9,8},{10,11... | collective-permute-start | bytes 2359304 | tf_op jit(solution)/shard_map/ppermute | solution.py:201
  52.4 0.5 weights.1
  52.9 1.0 %down.1 = f32[128,3072]{1,0:T(8,128)S(1)} custom-call(bf16[128,1024]{1,0:T(8,128)(2,1)S(1)} %hidden.1.hidden_ref, bf16[1,1024,3072]{2,1,0:T(8,128)(2,1)S(1)} %get-tuple-element.30.wd_ref), custom_call_target="tpu_custom_call" | custom-call | flops 805306368 | tf_op jit(solution)/shard_map/down/pallas_call | solution.py:29
  53.9 0.5 collective-permute-done.2
  54.4 0.2 fusion
  54.6 18.0 %all_to_all.11 = bf16[16,8,3072]{2,1,0:T(8,128)(2,1)S(1)} all-to-all(bf16[16,8,3072]{2,1,0:T(8,128)(2,1)S(1)} %fusion), channel_id=1, replica_groups=mesh['dp'=8,'x'=4,'zh'=2,'y'=4,'core'=2] {'x','y'}, dimensions={0} | all-to-all | bytes 1572864 | tf_op jit(solution)/shard_map/all_to_all | solution.py:228
  72.5 0.2 mix_other.1
  72.8 7.2 %collective-permute-start.3 = (bf16[8,3072]{1,0:T(8,128)(2,1)S(1)}, bf16[8,3072]{1,0:T(8,128)(2,1)S(1)}, u32[]{:S(2)}, u32[]{:S(2)}) collective-permute-start(bf16[8,3072]{1,0:T(8,128)(2,1)S(1)} %mix_other.1), channel_id=1, source_target_pairs={{0,8},{8,0},{1,9},{9,1},{2,10},{10,2},{3,11},{11,3},{4,12},{12,4},... | collective-permute-start | bytes 147464 | tf_op jit(solution)/shard_map/ppermute | solution.py:201
  80.0 0.2 mix_own.1
  80.2 8.4 %collective-permute-done.3 = bf16[8,3072]{1,0:T(8,128)(2,1)S(1)} collective-permute-done((bf16[8,3072]{1,0:T(8,128)(2,1)S(1)}, bf16[8,3072]{1,0:T(8,128)(2,1)S(1)}, u32[]{:S(2)}, u32[]{:S(2)}) %collective-permute-start.3) | collective-permute-done | bytes 49184 | tf_op jit(solution)/shard_map/ppermute | solution.py:201
  88.7 0.6 add_convert_fusion.1
Async XLA Ops:
  0.8 21.4 %collective-permute-start = (bf16[8,3200]{1,0:T(8,128)(2,1)S(1)}, bf16[8,3200]{1,0:T(8,128)(2,1)S(1)}, u32[]{:S(2)}, u32[]{:S(2)}) collective-permute-start(bf16[8,3200]{1,0:T(8,128)(2,1)S(1)} %pack.1.refs_0_.own_ref), channel_id=1, source_target_pairs={{0,8},{8,0},{1,9},{9,1},{2,10},{10,2},{3,11},{11,3},{4,12},{12,4},... | collective-permute-start | bytes 153608 | tf_op jit(solution)/shard_map/ppermute | solution.py:201
  43.3 4.2 %collective-permute-start.1 = (bf16[128,3072]{1,0:T(8,128)(2,1)S(1)}, bf16[128,3072]{1,0:T(8,128)(2,1)S(1)}, u32[]{:S(2)}, u32[]{:S(2)}) collective-permute-start(bf16[128,3072]{1,0:T(8,128)(2,1)S(1)} %bitcast.9), channel_id=1, source_target_pairs={{0,1},{1,0},{2,3},{3,2},{4,5},{5,4},{6,7},{7,6},{8,9},{9,8},{10,11... | collective-permute-start | bytes 2359304 | tf_op jit(solution)/shard_map/ppermute | solution.py:201
  50.2 4.2 %collective-permute-start.2 = (bf16[128,3072]{1,0:T(8,128)(2,1)S(1)}, bf16[128,3072]{1,0:T(8,128)(2,1)S(1)}, u32[]{:S(2)}, u32[]{:S(2)}) collective-permute-start(bf16[128,3072]{1,0:T(8,128)(2,1)S(1)} %expert.1), channel_id=1, source_target_pairs={{0,1},{1,0},{2,3},{3,2},{4,5},{5,4},{6,7},{7,6},{8,9},{9,8},{10,11... | collective-permute-start | bytes 2359304 | tf_op jit(solution)/shard_map/ppermute | solution.py:201
  72.8 15.9 %collective-permute-start.3 = (bf16[8,3072]{1,0:T(8,128)(2,1)S(1)}, bf16[8,3072]{1,0:T(8,128)(2,1)S(1)}, u32[]{:S(2)}, u32[]{:S(2)}) collective-permute-start(bf16[8,3072]{1,0:T(8,128)(2,1)S(1)} %mix_other.1), channel_id=1, source_target_pairs={{0,8},{8,0},{1,9},{9,1},{2,10},{10,2},{3,11},{11,3},{4,12},{12,4},... | collective-permute-start | bytes 147464 | tf_op jit(solution)/shard_map/ppermute | solution.py:201

commit v5 on v4

--- a/solution.py
+++ b/solution.py
@@ -195,6 +195,16 @@
 
 def mix(weights, rows, dtype, name):
     return call(mix_kernel, [((8, rows.shape[1]), dtype)], (weights, rows), name, flops=2 * weights.shape[0] * rows.size)[0]
+
+
+def both_kernel(own_ref, other_ref, rows_ref, keep_ref, send_ref):
+    total = dot(jnp.concatenate([own_ref[...], other_ref[...]], axis=0), rows_ref[...])
+    keep_ref[...] = total[0:8] + total[8:16] + total[16:24]
+    send_ref[...] = (total[24:32] + total[32:40] + total[40:48]).astype(BF16)
+
+
+def final_kernel(zh_ref, keep_ref, gathered_ref, out_ref):
+    out_ref[...] = (keep_ref[...] + gathered_ref[1 - zh_ref[0]].astype(F32)).astype(BF16)
 
 
 def swapped(value, axis):
@@ -226,10 +236,17 @@
     arrived, part, (own_weights, other_weights) = lax.optimization_barrier((arrived, part, mixers))
     pair = (part + arrived.astype(F32)).astype(BF16).reshape(slots.shape)
     back = lax.all_to_all(pair, ("x", "y"), 0, 0, tiled=True)
-    back = back.reshape(half, width)
-    arriving = swapped(mix(other_weights, back, BF16, "mix_other"), "zh")
-    keep = mix(own_weights, back, F32, "mix_own")
-    return (keep + arriving.astype(F32)).astype(BF16)
+    outs = [((8, width), F32), ((8, width), BF16)]
+    keep, send = call(both_kernel, outs, (own_weights, other_weights, back.reshape(half, width)), "mix")
+    gathered = lax.all_gather(send, "zh")
+    return pl.pallas_call(
+        final_kernel,
+        out_shape=jax.ShapeDtypeStruct((8, width), BF16),
+        in_specs=[pl.BlockSpec(memory_space=SMEM), pl.BlockSpec(memory_space=VMEM), pl.BlockSpec(memory_space=VMEM)],
+        out_specs=pl.BlockSpec(memory_space=VMEM),
+        compiler_params=pltpu.CompilerParams(vmem_limit_bytes=2**20),
+        name="final",
+    )(zh, pltpu.with_memory_space_constraint(keep, VMEM), pltpu.with_memory_space_constraint(gathered, VMEM))
 
 
 def solution(mesh):

time: 89.6 us -> 88.5 us (0.988)
  blocking collectives: 38.7 us -> 53.4 us
  waiting for transfers between devices: 9.24 us -> 0.83 us
  starting transfers between devices: 26.1 us -> 18.8 us
    all_gather x0 -> x1, blocking collectives: none -> 14.7 us  [on_device(): gathered = lax.all_gather(send, 'zh')]
    ppermute x4 -> x3, waiting for transfers between devices: 9.24 us -> 0.83 us  [swapped(): return lax.ppermute(value, axis, [(0, 1), (1, 0)])]
    ppermute x4 -> x3, starting transfers between devices: 26.1 us -> 18.8 us  [swapped(): return lax.ppermute(value, axis, [(0, 1), (1, 0)])]
    pallas_call x7 -> x6, Pallas kernels: 7.06 us -> 6.86 us  [call(): pl.pallas_call(kernel, out_shape=tuple((VMEM(shape, dtype) for shape, dty...]
  transfers between devices with their start and end apart: 4 -> 3, of which waited for: 3 -> 2; matrix products, arithmetic and copies ran while one was open for 0% -> 0% of each run, Pallas kernels for 11% -> 11%
where the time goes in v5:
time: 88.5 us; the launch traced here: 88.2 us
  blocking collectives  53.4 us (60%)
  starting transfers between devices  18.8 us (21%)
  Pallas kernels  14.9 us (17%)
    all_to_all x1, blocking collectives, on_device(): lax.all_to_all(slots, ('x', 'y'), 0, 0, tiled=True).reshape(half, width)  20.7 us
    ppermute x3, starting transfers between devices, swapped(): return lax.ppermute(value, axis, [(0, 1), (1, 0)])  18.8 us
    all_to_all x1, blocking collectives, on_device(): back = lax.all_to_all(pair, ('x', 'y'), 0, 0, tiled=True)  18 us
    all_gather x1, blocking collectives, on_device(): gathered = lax.all_gather(send, 'zh')  14.7 us
    pallas_call x6, Pallas kernels, call(): pl.pallas_call(kernel, out_shape=tuple((VMEM(shape, dtype) for shape, dty...  6.86 us
    pallas_call x1, Pallas kernels, loaded(): pl.pallas_call(load_kernel, out_shape=tuple((VMEM(w.shape, w.dtype) for w...  6.53 us
  transfers between devices with their start and end apart: 3, of which 2 were waited for; matrix products, arithmetic and copies ran while one was open for 0% of the time, Pallas kernels for 11%

profile of v5, /device:TPU:32, one launch (start us, length us, event | category | flops | bytes accessed | tf_op | source)
XLA Modules:
  0.0 88.2 jit_solution(12995321556603522404)
XLA Ops:
  0.0 0.8 pack.1.refs_0_.own_ref
  0.8 14.8 %collective-permute-start = (bf16[8,3200]{1,0:T(8,128)(2,1)S(1)}, bf16[8,3200]{1,0:T(8,128)(2,1)S(1)}, u32[]{:S(2)}, u32[]{:S(2)}) collective-permute-start(bf16[8,3200]{1,0:T(8,128)(2,1)S(1)} %pack.1.refs_0_.own_ref), channel_id=1, source_target_pairs={{0,8},{8,0},{1,9},{9,1},{2,10},{10,2},{3,11},{11,3},{4,12},{12,4},... | collective-permute-start | bytes 153608 | tf_op jit(solution)/shard_map/ppermute | solution.py:211
  15.7 6.5 %load.1 = (bf16[1,3072,1024]{2,1,0:T(8,128)(2,1)S(1)}, bf16[1,3072,1024]{2,1,0:T(8,128)(2,1)S(1)}, bf16[1,1024,3072]{2,1,0:T(8,128)(2,1)S(1)}) custom-call(bf16[8,3200]{1,0:T(8,128)(2,1)S(1)} %pack.1.refs_0_.own_ref, bf16[1,3072,1024]{2,1,0:T(8,128)(2,1)} %refs_1_.1, bf16[1,3072,1024]{2,1,0:T(8,128)(2,1)} %refs_2_.1, bf16[1,1024,3072]{2,1,0:T(8,128)(2,1)} %refs_3_.1), custom_call_target="tpu_custom_call" | custom-call | bytes 37748736 | tf_op jit(solution)/shard_map/load/pallas_call | solution.py:148
  22.2 0.0 collective-permute-done.other_ref
  22.2 0.4 place.1
  22.6 20.7 %all_to_all.10 = bf16[16,8,3072]{2,1,0:T(8,128)(2,1)S(1)} all-to-all(bf16[16,8,3072]{2,1,0:T(8,128)(2,1)S(1)} %place.1), channel_id=1, replica_groups=mesh['dp'=8,'x'=4,'zh'=2,'y'=4,'core'=2] {'x','y'}, dimensions={0} | all-to-all | bytes 1572864 | tf_op jit(solution)/shard_map/all_to_all | solution.py:224
  43.3 1.9 %collective-permute-start.1 = (bf16[128,3072]{1,0:T(8,128)(2,1)S(1)}, bf16[128,3072]{1,0:T(8,128)(2,1)S(1)}, u32[]{:S(2)}, u32[]{:S(2)}) collective-permute-start(bf16[128,3072]{1,0:T(8,128)(2,1)S(1)} %bitcast.9), channel_id=1, source_target_pairs={{0,1},{1,0},{2,3},{3,2},{4,5},{5,4},{6,7},{7,6},{8,9},{9,8},{10,11... | collective-permute-start | bytes 2359304 | tf_op jit(solution)/shard_map/ppermute | solution.py:211
  45.2 1.9 %hidden.1.hidden_ref = bf16[128,1024]{1,0:T(8,128)(2,1)S(1)} custom-call(bf16[128,3072]{1,0:T(8,128)(2,1)S(1)} %bitcast.10, bf16[1,3072,1024]{2,1,0:T(8,128)(2,1)S(1)} %get-tuple-element.29.wg_ref, bf16[1,3072,1024]{2,1,0:T(8,128)(2,1)S(1)} %get-tuple-element.30.wu_ref), custom_call_target="tpu_custom_call" | custom-call | flops 1610612736 | tf_op jit(solution)/shard_map/hidden/pallas_call | solution.py:29
  47.1 0.3 collective-permute-done.1.rows_ref
  47.4 2.8 %expert.1 = bf16[128,3072]{1,0:T(8,128)(2,1)S(1)} custom-call(bf16[128,3072]{1,0:T(8,128)(2,1)S(1)} %collective-permute-done.1.rows_ref, bf16[1,3072,1024]{2,1,0:T(8,128)(2,1)S(1)} %get-tuple-element.29.wg_ref, bf16[1,3072,1024]{2,1,0:T(8,128)(2,1)S(1)} %get-tuple-element.30.wu_ref, bf16[1,1024,3072]{2,1,0:T(8,128)(2,1)S(1)} %get-tuple-element.32.wd_ref), custom_call_target="tpu_custom_call" | custom-call | flops 2415919104 | tf_op jit(solution)/shard_map/expert/pallas_call | solution.py:29
  50.2 2.1 %collective-permute-start.2 = (bf16[128,3072]{1,0:T(8,128)(2,1)S(1)}, bf16[128,3072]{1,0:T(8,128)(2,1)S(1)}, u32[]{:S(2)}, u32[]{:S(2)}) collective-permute-start(bf16[128,3072]{1,0:T(8,128)(2,1)S(1)} %expert.1), channel_id=1, source_target_pairs={{0,1},{1,0},{2,3},{3,2},{4,5},{5,4},{6,7},{7,6},{8,9},{9,8},{10,11... | collective-permute-start | bytes 2359304 | tf_op jit(solution)/shard_map/ppermute | solution.py:211
  52.3 0.5 weights.1
  52.9 1.0 %down.1 = f32[128,3072]{1,0:T(8,128)S(1)} custom-call(bf16[128,1024]{1,0:T(8,128)(2,1)S(1)} %hidden.1.hidden_ref, bf16[1,1024,3072]{2,1,0:T(8,128)(2,1)S(1)} %get-tuple-element.32.wd_ref), custom_call_target="tpu_custom_call" | custom-call | flops 805306368 | tf_op jit(solution)/shard_map/down/pallas_call | solution.py:29
  53.9 0.5 collective-permute-done.2
  54.4 0.2 fusion
  54.6 18.0 %all_to_all.11 = bf16[16,8,3072]{2,1,0:T(8,128)(2,1)S(1)} all-to-all(bf16[16,8,3072]{2,1,0:T(8,128)(2,1)S(1)} %fusion), channel_id=1, replica_groups=mesh['dp'=8,'x'=4,'zh'=2,'y'=4,'core'=2] {'x','y'}, dimensions={0} | all-to-all | bytes 1572864 | tf_op jit(solution)/shard_map/all_to_all | solution.py:238
  72.5 0.2 mix.1
  72.8 14.7 %all-gather = bf16[16,3072]{1,0:T(8,128)(2,1)S(1)} all-gather(bf16[8,3072]{1,0:T(8,128)(2,1)S(1)} %get-tuple-element.44), channel_id=2, replica_groups=mesh['dp'=8,'x'=4,'zh'=2,'y'=4,'core'=2] {'zh'}, dimensions={0}, use_global_device_ids=true | all-gather | bytes 147456 | tf_op jit(solution)/shard_map/all_gather | solution.py:241
  87.5 0.6 final.1
Async XLA Ops:
  0.8 21.4 %collective-permute-start = (bf16[8,3200]{1,0:T(8,128)(2,1)S(1)}, bf16[8,3200]{1,0:T(8,128)(2,1)S(1)}, u32[]{:S(2)}, u32[]{:S(2)}) collective-permute-start(bf16[8,3200]{1,0:T(8,128)(2,1)S(1)} %pack.1.refs_0_.own_ref), channel_id=1, source_target_pairs={{0,8},{8,0},{1,9},{9,1},{2,10},{10,2},{3,11},{11,3},{4,12},{12,4},... | collective-permute-start | bytes 153608 | tf_op jit(solution)/shard_map/ppermute | solution.py:211
  43.3 4.2 %collective-permute-start.1 = (bf16[128,3072]{1,0:T(8,128)(2,1)S(1)}, bf16[128,3072]{1,0:T(8,128)(2,1)S(1)}, u32[]{:S(2)}, u32[]{:S(2)}) collective-permute-start(bf16[128,3072]{1,0:T(8,128)(2,1)S(1)} %bitcast.9), channel_id=1, source_target_pairs={{0,1},{1,0},{2,3},{3,2},{4,5},{5,4},{6,7},{7,6},{8,9},{9,8},{10,11... | collective-permute-start | bytes 2359304 | tf_op jit(solution)/shard_map/ppermute | solution.py:211
  50.2 4.2 %collective-permute-start.2 = (bf16[128,3072]{1,0:T(8,128)(2,1)S(1)}, bf16[128,3072]{1,0:T(8,128)(2,1)S(1)}, u32[]{:S(2)}, u32[]{:S(2)}) collective-permute-start(bf16[128,3072]{1,0:T(8,128)(2,1)S(1)} %expert.1), channel_id=1, source_target_pairs={{0,1},{1,0},{2,3},{3,2},{4,5},{5,4},{6,7},{7,6},{8,9},{9,8},{10,11... | collective-permute-start | bytes 2359304 | tf_op jit(solution)/shard_map/ppermute | solution.py:211

commit v6 on v5

--- a/solution.py
+++ b/solution.py
@@ -80,22 +80,22 @@
     return jnp.where(mine & (named > 0.5) & (rank == (r % SLOTS).astype(F32)), 1.0, 0.0).astype(BF16)
 
 
-def place_kernel(zh_ref, own_ref, other_ref, out_ref, both_ref):
+def place_kernel(zh_ref, own_ref, halves_ref, out_ref, both_ref):
     width = out_ref.shape[-1]
     zh = zh_ref[0]
     both_ref[0:8] = own_ref[:, :width]
-    both_ref[8:16] = other_ref[:, :width]
-    places = [placement(own_ref[:, width:], zh, 0), placement(other_ref[:, width:], zh, 1)]
+    both_ref[8:16] = halves_ref[1 - zh, :, :width]
+    places = [placement(own_ref[:, width:], zh, 0), placement(halves_ref[1 - zh, :, width:], zh, 1)]
     slots = dot(jnp.concatenate(places, axis=1), both_ref[...]).astype(BF16)
     for x in range(X):
         for y in range(Y):
             out_ref[x * Y + y] = slots[x * 2 * SLOTS : (x + 1) * 2 * SLOTS]
 
 
-def placed(zh, own, other):
+def placed(zh, own, halves):
     width = own.shape[1] - META
     outs = [((X * Y, 2 * SLOTS, width), BF16)]
-    return call(place_kernel, outs, (zh, own, other), "place", [pltpu.VMEM((16, width), BF16)])[0]
+    return call(place_kernel, outs, (zh, own, halves), "place", [pltpu.VMEM((16, width), BF16)], flops=2**35)[0]
 
 
 BLOCK = 256
@@ -124,37 +124,6 @@
 def expert_kernel(rows_ref, wg_ref, wu_ref, wd_ref, out_ref, hidden_ref):
     hidden_units(rows_ref[...], wg_ref, wu_ref, hidden_ref)
     down(hidden_ref[...], wd_ref, out_ref)
-
-
-PIECES = 4
-
-
-def load_kernel(*refs):
-    sources, targets, sems = refs[1:4], refs[4:7], refs[7]
-    copies = []
-    for source, target in zip(sources, targets):
-        rows = source.shape[1] // PIECES
-        for piece in range(PIECES):
-            part = pl.ds(piece * rows, rows)
-            copies.append(pltpu.make_async_copy(source.at[0, part], target.at[0, part], sems.at[len(copies)]))
-    for copy in copies:
-        copy.start()
-    for copy in copies:
-        copy.wait()
-
-
-def loaded(after, *weights):
-    anywhere = pl.BlockSpec(memory_space=pl.ANY)
-    return pl.pallas_call(
-        load_kernel,
-        out_shape=tuple(VMEM(w.shape, w.dtype) for w in weights),
-        in_specs=[anywhere] * (1 + len(weights)),
-        out_specs=tuple(pl.BlockSpec(memory_space=VMEM) for _ in weights),
-        scratch_shapes=[pltpu.SemaphoreType.DMA((len(weights) * PIECES,))],
-        cost_estimate=pl.CostEstimate(flops=0, transcendentals=0, bytes_accessed=2 * sum(w.size * 2 for w in weights)),
-        compiler_params=pltpu.CompilerParams(vmem_limit_bytes=2**20),
-        name="load",
-    )(after, *in_hbm(*weights))
 
 
 def mixing(meta, zh, block):
@@ -182,10 +151,10 @@
     return jnp.concatenate([high, mid, weights - high - mid], axis=0).astype(BF16)
 
 
-def weights_kernel(zh_ref, own_ref, other_ref, own_out, other_out):
+def weights_kernel(zh_ref, own_ref, halves_ref, own_out, other_out):
     width = own_ref.shape[1] - META
     own_out[...] = split(mixing(own_ref[:, width:], zh_ref[0], 0))
-    other_out[...] = split(mixing(other_ref[:, width:], zh_ref[0], 1))
+    other_out[...] = split(mixing(halves_ref[1 - zh_ref[0], :, width:], zh_ref[0], 1))
 
 
 def mix_kernel(weights_ref, rows_ref, out_ref):
@@ -216,10 +185,9 @@
     units = gate_proj.shape[2]
     zh = lax.axis_index("zh").astype(jnp.int32).reshape(1)
     own = packed(tokens, expert_ids, gate_weights)
-    other = swapped(own, "zh")
-    weights = loaded(own, gate_proj, up_proj, down_proj)
-    other, (wg, wu, wd) = lax.optimization_barrier((other, weights))
-    slots = placed(zh, own, other)
+    halves = lax.all_gather(own, "zh")
+    wg, wu, wd = gate_proj, up_proj, down_proj
+    slots = placed(zh, own, halves)
     half = slots.shape[0] * slots.shape[1]
     rows = lax.all_to_all(slots, ("x", "y"), 0, 0, tiled=True).reshape(half, width)
     core_rows = swapped(rows, "core")
@@ -228,11 +196,11 @@
     core_rows, hidden = lax.optimization_barrier((core_rows, hidden))
     scratch = [pltpu.VMEM((half, units), BF16)]
     core_part = call(expert_kernel, [((half, width), BF16)], (core_rows, wg, wu, wd), "expert", scratch, flops=3 * third)[0]
-    core_part, own, other = lax.optimization_barrier((core_part, own, other))
+    core_part, own, halves = lax.optimization_barrier((core_part, own, halves))
     arrived = swapped(core_part, "core")
     part = call(down_kernel, [((half, width), F32)], (hidden, wd), "down", flops=third)[0]
     outs = [((24, half), BF16), ((24, half), BF16)]
-    mixers = call(weights_kernel, outs, (zh, own, other), "weights", flops=2**28)
+    mixers = call(weights_kernel, outs, (zh, own, halves), "weights", flops=2**28)
     arrived, part, (own_weights, other_weights) = lax.optimization_barrier((arrived, part, mixers))
     pair = (part + arrived.astype(F32)).astype(BF16).reshape(slots.shape)
     back = lax.all_to_all(pair, ("x", "y"), 0, 0, tiled=True)

time: 88.5 us -> 82.2 us (0.929)
  the two profiles are of different devices: /device:TPU:32 before, /device:TPU:192 now
where the time goes in v6:
time: 82.2 us; the launch traced here: 81.9 us
  blocking collectives  68.3 us (83%)
  Pallas kernels  8.35 us (10%)
  starting transfers between devices  4.27 us (5%)
    all_to_all x1, blocking collectives, on_device(): lax.all_to_all(slots, ('x', 'y'), 0, 0, tiled=True).reshape(half, width)  21.8 us
    all_to_all x1, blocking collectives, on_device(): back = lax.all_to_all(pair, ('x', 'y'), 0, 0, tiled=True)  18.1 us
    all_gather x1, blocking collectives, on_device(): halves = lax.all_gather(own, 'zh')  14.9 us
    all_gather x1, blocking collectives, on_device(): gathered = lax.all_gather(send, 'zh')  13.5 us
    pallas_call x6, Pallas kernels, call(): pl.pallas_call(kernel, out_shape=tuple((VMEM(shape, dtype) for shape, dty...  6.88 us
    ppermute x2, starting transfers between devices, swapped(): return lax.ppermute(value, axis, [(0, 1), (1, 0)])  4.27 us
  transfers between devices with their start and end apart: 2, of which 2 were waited for; matrix products, arithmetic and copies ran while one was open for 0% of the time, Pallas kernels for 4%

profile of v6, /device:TPU:192, one launch (start us, length us, event | category | flops | bytes accessed | tf_op | source)
XLA Modules:
  0.0 81.9 jit_solution(4826547518696485206)
XLA Ops:
  0.0 0.8 %pack.1.own_ref = bf16[8,3200]{1,0:T(8,128)(2,1)S(1)} custom-call(bf16[8,3072]{1,0:T(8,128)(2,1)} %tok_ref.1, s32[2,8]{1,0:T(2,128)} %bitcast.21, f32[2,8]{1,0:T(2,128)} %bitcast.22), custom_call_target="tpu_custom_call" | custom-call | tf_op jit(solution)/shard_map/pack/pallas_call | solution.py:61
  0.8 14.9 %all-gather = bf16[16,3200]{1,0:T(8,128)(2,1)S(1)} all-gather(bf16[8,3200]{1,0:T(8,128)(2,1)S(1)} %pack.1.own_ref), channel_id=2, replica_groups=mesh['dp'=8,'x'=4,'zh'=2,'y'=4,'core'=2] {'zh'}, dimensions={0}, use_global_device_ids=true | all-gather | bytes 153600 | tf_op jit(solution)/shard_map/all_gather | solution.py:188
  15.8 0.0 slice-start
  15.8 0.0 slice-start.2
  15.8 0.0 slice-start.1
  15.8 0.0 slice-start.3
  15.8 0.4 place.1
  16.2 0.0 slice-start.4
  16.2 21.8 %all_to_all.10 = bf16[16,8,3072]{2,1,0:T(8,128)(2,1)S(1)} all-to-all(bf16[16,8,3072]{2,1,0:T(8,128)(2,1)S(1)} %place.1), channel_id=1, replica_groups=mesh['dp'=8,'x'=4,'zh'=2,'y'=4,'core'=2] {'x','y'}, dimensions={0} | all-to-all | bytes 1572864 | tf_op jit(solution)/shard_map/all_to_all | solution.py:192
  38.0 0.0 slice-start.5
  38.0 2.0 %collective-permute-start = (bf16[128,3072]{1,0:T(8,128)(2,1)S(1)}, bf16[128,3072]{1,0:T(8,128)(2,1)S(1)}, u32[]{:S(2)}, u32[]{:S(2)}) collective-permute-start(bf16[128,3072]{1,0:T(8,128)(2,1)S(1)} %bitcast.16), channel_id=1, source_target_pairs={{0,1},{1,0},{2,3},{3,2},{4,5},{5,4},{6,7},{7,6},{8,9},{9,8},{10,11... | collective-permute-start | bytes 2359304 | tf_op jit(solution)/shard_map/ppermute | solution.py:180
  40.1 0.0 slice-done
  40.1 0.0 slice-done.2
  40.1 0.0 slice-done.1
  40.1 0.0 slice-done.3
  40.1 2.0 %hidden.1.hidden_ref = bf16[128,1024]{1,0:T(8,128)(2,1)S(1)} custom-call(bf16[128,3072]{1,0:T(8,128)(2,1)S(1)} %bitcast.17, bf16[1,3072,1024]{2,1,0:T(8,128)(2,1)S(1)} %bitcast.10, bf16[1,3072,1024]{2,1,0:T(8,128)(2,1)S(1)} %bitcast.12), custom_call_target="tpu_custom_call" | custom-call | flops 1610612736 | tf_op jit(solution)/shard_map/hidden/pallas_call | solution.py:29
  42.1 0.2 collective-permute-done.rows_ref
  42.3 0.0 slice-done.4
  42.3 0.0 slice-done.5
  42.3 2.8 %expert.1 = bf16[128,3072]{1,0:T(8,128)(2,1)S(1)} custom-call(bf16[128,3072]{1,0:T(8,128)(2,1)S(1)} %collective-permute-done.rows_ref, bf16[1,3072,1024]{2,1,0:T(8,128)(2,1)S(1)} %bitcast.10, bf16[1,3072,1024]{2,1,0:T(8,128)(2,1)S(1)} %bitcast.12, bf16[1,1024,3072]{2,1,0:T(8,128)(2,1)S(1)} %bitcast.14), custom_call_target="tpu_custom_call" | custom-call | flops 2415919104 | tf_op jit(solution)/shard_map/expert/pallas_call | solution.py:29
  45.1 2.2 %collective-permute-start.1 = (bf16[128,3072]{1,0:T(8,128)(2,1)S(1)}, bf16[128,3072]{1,0:T(8,128)(2,1)S(1)}, u32[]{:S(2)}, u32[]{:S(2)}) collective-permute-start(bf16[128,3072]{1,0:T(8,128)(2,1)S(1)} %expert.1), channel_id=1, source_target_pairs={{0,1},{1,0},{2,3},{3,2},{4,5},{5,4},{6,7},{7,6},{8,9},{9,8},{10,11... | collective-permute-start | bytes 2359304 | tf_op jit(solution)/shard_map/ppermute | solution.py:180
  47.3 0.5 weights.1
  47.8 1.0 %down.1 = f32[128,3072]{1,0:T(8,128)S(1)} custom-call(bf16[128,1024]{1,0:T(8,128)(2,1)S(1)} %hidden.1.hidden_ref, bf16[1,1024,3072]{2,1,0:T(8,128)(2,1)S(1)} %bitcast.14), custom_call_target="tpu_custom_call" | custom-call | flops 805306368 | tf_op jit(solution)/shard_map/down/pallas_call | solution.py:29
  48.9 0.4 collective-permute-done.1
  49.3 0.2 fusion
  49.5 18.1 %all_to_all.11 = bf16[16,8,3072]{2,1,0:T(8,128)(2,1)S(1)} all-to-all(bf16[16,8,3072]{2,1,0:T(8,128)(2,1)S(1)} %fusion), channel_id=1, replica_groups=mesh['dp'=8,'x'=4,'zh'=2,'y'=4,'core'=2] {'x','y'}, dimensions={0} | all-to-all | bytes 1572864 | tf_op jit(solution)/shard_map/all_to_all | solution.py:206
  67.6 0.2 mix.1
  67.8 13.5 %all-gather.1 = bf16[16,3072]{1,0:T(8,128)(2,1)S(1)} all-gather(bf16[8,3072]{1,0:T(8,128)(2,1)S(1)} %get-tuple-element.30), channel_id=3, replica_groups=mesh['dp'=8,'x'=4,'zh'=2,'y'=4,'core'=2] {'zh'}, dimensions={0}, use_global_device_ids=true | all-gather | bytes 147456 | tf_op jit(solution)/shard_map/all_gather | solution.py:209
  81.3 0.6 final.1
  (3 shorter events, 0.0 us)
Async XLA Ops:
  15.8 24.3 %slice-start = ((s8[6291456]{0:T(1024)(128)(4,1)}), s8[4194304]{0:T(1024)(128)(4,1)S(1)}, s32[]{:S(2)}) async-start(s8[6291456]{0:T(1024)(128)(4,1)} %bitcast.9), calls=%async_computation.2 | async-start | bytes 8388608
  15.8 24.3 %slice-start.2 = ((s8[6291456]{0:T(1024)(128)(4,1)}), s8[4194304]{0:T(1024)(128)(4,1)S(1)}, s32[]{:S(2)}) async-start(s8[6291456]{0:T(1024)(128)(4,1)} %bitcast.11), calls=%async_computation.4 | async-start | bytes 8388608
  15.8 24.3 %slice-start.1 = ((s8[6291456]{0:T(1024)(128)(4,1)}), s8[2097152]{0:T(1024)(128)(4,1)S(1)}, s32[]{:S(2)}) async-start(s8[6291456]{0:T(1024)(128)(4,1)} %bitcast.9), calls=%async_computation.3 | async-start | bytes 4194304
  15.8 24.3 %slice-start.3 = ((s8[6291456]{0:T(1024)(128)(4,1)}), s8[2097152]{0:T(1024)(128)(4,1)S(1)}, s32[]{:S(2)}) async-start(s8[6291456]{0:T(1024)(128)(4,1)} %bitcast.11), calls=%async_computation.5 | async-start | bytes 4194304
  16.2 26.2 %slice-start.4 = ((s8[6291456]{0:T(1024)(128)(4,1)}), s8[4194304]{0:T(1024)(128)(4,1)S(1)}, s32[]{:S(2)}) async-start(s8[6291456]{0:T(1024)(128)(4,1)} %bitcast.13), calls=%async_computation.6 | async-start | bytes 8388608
  38.0 4.3 %slice-start.5 = ((s8[6291456]{0:T(1024)(128)(4,1)}), s8[2097152]{0:T(1024)(128)(4,1)S(1)}, s32[]{:S(2)}) async-start(s8[6291456]{0:T(1024)(128)(4,1)} %bitcast.13), calls=%async_computation.7 | async-start | bytes 4194304
  38.0 4.3 %collective-permute-start = (bf16[128,3072]{1,0:T(8,128)(2,1)S(1)}, bf16[128,3072]{1,0:T(8,128)(2,1)S(1)}, u32[]{:S(2)}, u32[]{:S(2)}) collective-permute-start(bf16[128,3072]{1,0:T(8,128)(2,1)S(1)} %bitcast.16), channel_id=1, source_target_pairs={{0,1},{1,0},{2,3},{3,2},{4,5},{5,4},{6,7},{7,6},{8,9},{9,8},{10,11... | collective-permute-start | bytes 2359304 | tf_op jit(solution)/shard_map/ppermute | solution.py:180
  45.1 4.2 %collective-permute-start.1 = (bf16[128,3072]{1,0:T(8,128)(2,1)S(1)}, bf16[128,3072]{1,0:T(8,128)(2,1)S(1)}, u32[]{:S(2)}, u32[]{:S(2)}) collective-permute-start(bf16[128,3072]{1,0:T(8,128)(2,1)S(1)} %expert.1), channel_id=1, source_target_pairs={{0,1},{1,0},{2,3},{3,2},{4,5},{5,4},{6,7},{7,6},{8,9},{9,8},{10,11... | collective-permute-start | bytes 2359304 | tf_op jit(solution)/shard_map/ppermute | solution.py:180

commit v7 on v6

--- a/solution.py
+++ b/solution.py
@@ -98,7 +98,7 @@
     return call(place_kernel, outs, (zh, own, halves), "place", [pltpu.VMEM((16, width), BF16)], flops=2**35)[0]
 
 
-BLOCK = 256
+BLOCK = 512
 
 
 def hidden_units(rows, wg_ref, wu_ref, out_ref):

time: 82.2 us -> 82 us (level)
  no operation moved by 1% of the time
where the time goes in v7:
time: 82 us; the launch traced here: 81.7 us
  blocking collectives  68.2 us (83%)
  Pallas kernels  8.14 us (10%)
  starting transfers between devices  4.1 us (5%)
  waiting for transfers between devices  0.96 us (1%)
    all_to_all x1, blocking collectives, on_device(): lax.all_to_all(slots, ('x', 'y'), 0, 0, tiled=True).reshape(half, width)  21.8 us
    all_to_all x1, blocking collectives, on_device(): back = lax.all_to_all(pair, ('x', 'y'), 0, 0, tiled=True)  17.9 us
    all_gather x1, blocking collectives, on_device(): halves = lax.all_gather(own, 'zh')  14.9 us
    all_gather x1, blocking collectives, on_device(): gathered = lax.all_gather(send, 'zh')  13.5 us
    pallas_call x6, Pallas kernels, call(): pl.pallas_call(kernel, out_shape=tuple((VMEM(shape, dtype) for shape, dty...  6.67 us
    ppermute x2, starting transfers between devices, swapped(): return lax.ppermute(value, axis, [(0, 1), (1, 0)])  4.1 us
  transfers between devices with their start and end apart: 2, of which 2 were waited for; matrix products, arithmetic and copies ran while one was open for 0% of the time, Pallas kernels for 4%

profile of v7, /device:TPU:192, one launch (start us, length us, event | category | flops | bytes accessed | tf_op | source)
XLA Modules:
  0.0 81.7 jit_solution(6606874851982082066)
XLA Ops:
  0.0 0.8 %pack.1.own_ref = bf16[8,3200]{1,0:T(8,128)(2,1)S(1)} custom-call(bf16[8,3072]{1,0:T(8,128)(2,1)} %tok_ref.1, s32[2,8]{1,0:T(2,128)} %bitcast.21, f32[2,8]{1,0:T(2,128)} %bitcast.22), custom_call_target="tpu_custom_call" | custom-call | tf_op jit(solution)/shard_map/pack/pallas_call | solution.py:61
  0.8 14.9 %all-gather = bf16[16,3200]{1,0:T(8,128)(2,1)S(1)} all-gather(bf16[8,3200]{1,0:T(8,128)(2,1)S(1)} %pack.1.own_ref), channel_id=2, replica_groups=mesh['dp'=8,'x'=4,'zh'=2,'y'=4,'core'=2] {'zh'}, dimensions={0}, use_global_device_ids=true | all-gather | bytes 153600 | tf_op jit(solution)/shard_map/all_gather | solution.py:188
  15.8 0.0 slice-start
  15.8 0.0 slice-start.2
  15.8 0.0 slice-start.1
  15.8 0.0 slice-start.3
  15.8 0.4 place.1
  16.2 0.0 slice-start.4
  16.2 21.8 %all_to_all.10 = bf16[16,8,3072]{2,1,0:T(8,128)(2,1)S(1)} all-to-all(bf16[16,8,3072]{2,1,0:T(8,128)(2,1)S(1)} %place.1), channel_id=1, replica_groups=mesh['dp'=8,'x'=4,'zh'=2,'y'=4,'core'=2] {'x','y'}, dimensions={0} | all-to-all | bytes 1572864 | tf_op jit(solution)/shard_map/all_to_all | solution.py:192
  38.0 0.0 slice-start.5
  38.0 2.0 %collective-permute-start = (bf16[128,3072]{1,0:T(8,128)(2,1)S(1)}, bf16[128,3072]{1,0:T(8,128)(2,1)S(1)}, u32[]{:S(2)}, u32[]{:S(2)}) collective-permute-start(bf16[128,3072]{1,0:T(8,128)(2,1)S(1)} %bitcast.16), channel_id=1, source_target_pairs={{0,1},{1,0},{2,3},{3,2},{4,5},{5,4},{6,7},{7,6},{8,9},{9,8},{10,11... | collective-permute-start | bytes 2359304 | tf_op jit(solution)/shard_map/ppermute | solution.py:180
  40.1 0.0 slice-done
  40.1 0.0 slice-done.2
  40.1 0.0 slice-done.1
  40.1 0.0 slice-done.3
  40.1 1.8 %hidden.1.hidden_ref = bf16[128,1024]{1,0:T(8,128)(2,1)S(1)} custom-call(bf16[128,3072]{1,0:T(8,128)(2,1)S(1)} %bitcast.17, bf16[1,3072,1024]{2,1,0:T(8,128)(2,1)S(1)} %bitcast.10, bf16[1,3072,1024]{2,1,0:T(8,128)(2,1)S(1)} %bitcast.12), custom_call_target="tpu_custom_call" | custom-call | flops 1610612736 | tf_op jit(solution)/shard_map/hidden/pallas_call | solution.py:29
  41.9 0.4 collective-permute-done.rows_ref
  42.3 0.0 slice-done.4
  42.3 0.0 slice-done.5
  42.3 2.7 %expert.1 = bf16[128,3072]{1,0:T(8,128)(2,1)S(1)} custom-call(bf16[128,3072]{1,0:T(8,128)(2,1)S(1)} %collective-permute-done.rows_ref, bf16[1,3072,1024]{2,1,0:T(8,128)(2,1)S(1)} %bitcast.10, bf16[1,3072,1024]{2,1,0:T(8,128)(2,1)S(1)} %bitcast.12, bf16[1,1024,3072]{2,1,0:T(8,128)(2,1)S(1)} %bitcast.14), custom_call_target="tpu_custom_call" | custom-call | flops 2415919104 | tf_op jit(solution)/shard_map/expert/pallas_call | solution.py:29
  45.0 2.1 %collective-permute-start.1 = (bf16[128,3072]{1,0:T(8,128)(2,1)S(1)}, bf16[128,3072]{1,0:T(8,128)(2,1)S(1)}, u32[]{:S(2)}, u32[]{:S(2)}) collective-permute-start(bf16[128,3072]{1,0:T(8,128)(2,1)S(1)} %expert.1), channel_id=1, source_target_pairs={{0,1},{1,0},{2,3},{3,2},{4,5},{5,4},{6,7},{7,6},{8,9},{9,8},{10,11... | collective-permute-start | bytes 2359304 | tf_op jit(solution)/shard_map/ppermute | solution.py:180
  47.1 0.5 weights.1
  47.6 1.0 %down.1 = f32[128,3072]{1,0:T(8,128)S(1)} custom-call(bf16[128,1024]{1,0:T(8,128)(2,1)S(1)} %hidden.1.hidden_ref, bf16[1,1024,3072]{2,1,0:T(8,128)(2,1)S(1)} %bitcast.14), custom_call_target="tpu_custom_call" | custom-call | flops 805306368 | tf_op jit(solution)/shard_map/down/pallas_call | solution.py:29
  48.6 0.6 collective-permute-done.1
  49.2 0.2 fusion
  49.4 17.9 %all_to_all.11 = bf16[16,8,3072]{2,1,0:T(8,128)(2,1)S(1)} all-to-all(bf16[16,8,3072]{2,1,0:T(8,128)(2,1)S(1)} %fusion), channel_id=1, replica_groups=mesh['dp'=8,'x'=4,'zh'=2,'y'=4,'core'=2] {'x','y'}, dimensions={0} | all-to-all | bytes 1572864 | tf_op jit(solution)/shard_map/all_to_all | solution.py:206
  67.3 0.2 mix.1
  67.6 13.5 %all-gather.1 = bf16[16,3072]{1,0:T(8,128)(2,1)S(1)} all-gather(bf16[8,3072]{1,0:T(8,128)(2,1)S(1)} %get-tuple-element.30), channel_id=3, replica_groups=mesh['dp'=8,'x'=4,'zh'=2,'y'=4,'core'=2] {'zh'}, dimensions={0}, use_global_device_ids=true | all-gather | bytes 147456 | tf_op jit(solution)/shard_map/all_gather | solution.py:209
  81.1 0.6 final.1
  (3 shorter events, 0.0 us)
Async XLA Ops:
  15.8 24.3 %slice-start = ((s8[6291456]{0:T(1024)(128)(4,1)}), s8[4194304]{0:T(1024)(128)(4,1)S(1)}, s32[]{:S(2)}) async-start(s8[6291456]{0:T(1024)(128)(4,1)} %bitcast.9), calls=%async_computation.2 | async-start | bytes 8388608
  15.8 24.3 %slice-start.2 = ((s8[6291456]{0:T(1024)(128)(4,1)}), s8[4194304]{0:T(1024)(128)(4,1)S(1)}, s32[]{:S(2)}) async-start(s8[6291456]{0:T(1024)(128)(4,1)} %bitcast.11), calls=%async_computation.4 | async-start | bytes 8388608
  15.8 24.3 %slice-start.1 = ((s8[6291456]{0:T(1024)(128)(4,1)}), s8[2097152]{0:T(1024)(128)(4,1)S(1)}, s32[]{:S(2)}) async-start(s8[6291456]{0:T(1024)(128)(4,1)} %bitcast.9), calls=%async_computation.3 | async-start | bytes 4194304
  15.8 24.3 %slice-start.3 = ((s8[6291456]{0:T(1024)(128)(4,1)}), s8[2097152]{0:T(1024)(128)(4,1)S(1)}, s32[]{:S(2)}) async-start(s8[6291456]{0:T(1024)(128)(4,1)} %bitcast.11), calls=%async_computation.5 | async-start | bytes 4194304
  16.2 26.2 %slice-start.4 = ((s8[6291456]{0:T(1024)(128)(4,1)}), s8[4194304]{0:T(1024)(128)(4,1)S(1)}, s32[]{:S(2)}) async-start(s8[6291456]{0:T(1024)(128)(4,1)} %bitcast.13), calls=%async_computation.6 | async-start | bytes 8388608
  38.0 4.3 %slice-start.5 = ((s8[6291456]{0:T(1024)(128)(4,1)}), s8[2097152]{0:T(1024)(128)(4,1)S(1)}, s32[]{:S(2)}) async-start(s8[6291456]{0:T(1024)(128)(4,1)} %bitcast.13), calls=%async_computation.7 | async-start | bytes 4194304
  38.0 4.3 %collective-permute-start = (bf16[128,3072]{1,0:T(8,128)(2,1)S(1)}, bf16[128,3072]{1,0:T(8,128)(2,1)S(1)}, u32[]{:S(2)}, u32[]{:S(2)}) collective-permute-start(bf16[128,3072]{1,0:T(8,128)(2,1)S(1)} %bitcast.16), channel_id=1, source_target_pairs={{0,1},{1,0},{2,3},{3,2},{4,5},{5,4},{6,7},{7,6},{8,9},{9,8},{10,11... | collective-permute-start | bytes 2359304 | tf_op jit(solution)/shard_map/ppermute | solution.py:180
  45.0 4.2 %collective-permute-start.1 = (bf16[128,3072]{1,0:T(8,128)(2,1)S(1)}, bf16[128,3072]{1,0:T(8,128)(2,1)S(1)}, u32[]{:S(2)}, u32[]{:S(2)}) collective-permute-start(bf16[128,3072]{1,0:T(8,128)(2,1)S(1)} %expert.1), channel_id=1, source_target_pairs={{0,1},{1,0},{2,3},{3,2},{4,5},{5,4},{6,7},{7,6},{8,9},{9,8},{10,11... | collective-permute-start | bytes 2359304 | tf_op jit(solution)/shard_map/ppermute | solution.py:180

commit v8 on v7

--- a/solution.py
+++ b/solution.py
@@ -64,6 +64,7 @@
         out_specs=pl.BlockSpec(memory_space=VMEM),
         scratch_shapes=[pltpu.VMEM((8, META), F32)],
         compiler_params=pltpu.CompilerParams(vmem_limit_bytes=2**20),
+        cost_estimate=pl.CostEstimate(flops=2**35, transcendentals=0, bytes_accessed=0),
         name="pack",
     )(*in_hbm(tokens, ids.T, gate_weights.T))
 
@@ -95,7 +96,7 @@
 def placed(zh, own, halves):
     width = own.shape[1] - META
     outs = [((X * Y, 2 * SLOTS, width), BF16)]
-    return call(place_kernel, outs, (zh, own, halves), "place", [pltpu.VMEM((16, width), BF16)], flops=2**35)[0]
+    return call(place_kernel, outs, (zh, own, halves), "place", [pltpu.VMEM((16, width), BF16)])[0]
 
 
 BLOCK = 512
@@ -155,15 +156,6 @@
     width = own_ref.shape[1] - META
     own_out[...] = split(mixing(own_ref[:, width:], zh_ref[0], 0))
     other_out[...] = split(mixing(halves_ref[1 - zh_ref[0], :, width:], zh_ref[0], 1))
-
-
-def mix_kernel(weights_ref, rows_ref, out_ref):
-    total = dot(weights_ref[...], rows_ref[...])
-    out_ref[...] = (total[0:8] + total[8:16] + total[16:24]).astype(out_ref.dtype)
-
-
-def mix(weights, rows, dtype, name):
-    return call(mix_kernel, [((8, rows.shape[1]), dtype)], (weights, rows), name, flops=2 * weights.shape[0] * rows.size)[0]
 
 
 def both_kernel(own_ref, other_ref, rows_ref, keep_ref, send_ref):

time: 82 us -> 82.2 us (level)
  no operation moved by 1% of the time
where the time goes in v8:
time: 82.2 us; the launch traced here: 82 us
  blocking collectives  68.3 us (83%)
  Pallas kernels  8.28 us (10%)
  starting transfers between devices  4.09 us (5%)
  waiting for transfers between devices  0.96 us (1%)
    all_to_all x1, blocking collectives, on_device(): lax.all_to_all(slots, ('x', 'y'), 0, 0, tiled=True).reshape(half, width)  21.9 us
    all_to_all x1, blocking collectives, on_device(): back = lax.all_to_all(pair, ('x', 'y'), 0, 0, tiled=True)  17.9 us
    all_gather x1, blocking collectives, on_device(): halves = lax.all_gather(own, 'zh')  15.1 us
    all_gather x1, blocking collectives, on_device(): gathered = lax.all_gather(send, 'zh')  13.5 us
    pallas_call x6, Pallas kernels, call(): pl.pallas_call(kernel, out_shape=tuple((VMEM(shape, dtype) for shape, dty...  6.67 us
    ppermute x2, starting transfers between devices, swapped(): return lax.ppermute(value, axis, [(0, 1), (1, 0)])  4.09 us
  transfers between devices with their start and end apart: 2, of which 2 were waited for; matrix products, arithmetic and copies ran while one was open for 0% of the time, Pallas kernels for 4%

profile of v8, /device:TPU:192, one launch (start us, length us, event | category | flops | bytes accessed | tf_op | source)
XLA Modules:
  0.0 82.0 jit_solution(6581564697877699008)
XLA Ops:
  0.0 0.0 slice-start
  0.0 0.0 slice-start.2
  0.0 0.0 slice-start.1
  0.0 0.0 slice-start.3
  0.0 1.0 %pack.1.own_ref = bf16[8,3200]{1,0:T(8,128)(2,1)S(1)} custom-call(bf16[8,3072]{1,0:T(8,128)(2,1)} %tok_ref.1, s32[2,8]{1,0:T(2,128)} %bitcast.21, f32[2,8]{1,0:T(2,128)} %bitcast.22), custom_call_target="tpu_custom_call" | custom-call | flops 34359738368 | tf_op jit(solution)/shard_map/pack/pallas_call | solution.py:61
  1.0 15.1 %all-gather = bf16[16,3200]{1,0:T(8,128)(2,1)S(1)} all-gather(bf16[8,3200]{1,0:T(8,128)(2,1)S(1)} %pack.1.own_ref), channel_id=2, replica_groups=mesh['dp'=8,'x'=4,'zh'=2,'y'=4,'core'=2] {'zh'}, dimensions={0}, use_global_device_ids=true | all-gather | bytes 153600 | tf_op jit(solution)/shard_map/all_gather | solution.py:180
  16.1 0.4 place.1
  16.4 0.0 slice-start.4
  16.5 21.9 %all_to_all.10 = bf16[16,8,3072]{2,1,0:T(8,128)(2,1)S(1)} all-to-all(bf16[16,8,3072]{2,1,0:T(8,128)(2,1)S(1)} %place.1), channel_id=1, replica_groups=mesh['dp'=8,'x'=4,'zh'=2,'y'=4,'core'=2] {'x','y'}, dimensions={0} | all-to-all | bytes 1572864 | tf_op jit(solution)/shard_map/all_to_all | solution.py:184
  38.3 0.0 slice-start.5
  38.3 2.0 %collective-permute-start = (bf16[128,3072]{1,0:T(8,128)(2,1)S(1)}, bf16[128,3072]{1,0:T(8,128)(2,1)S(1)}, u32[]{:S(2)}, u32[]{:S(2)}) collective-permute-start(bf16[128,3072]{1,0:T(8,128)(2,1)S(1)} %bitcast.16), channel_id=1, source_target_pairs={{0,1},{1,0},{2,3},{3,2},{4,5},{5,4},{6,7},{7,6},{8,9},{9,8},{10,11... | collective-permute-start | bytes 2359304 | tf_op jit(solution)/shard_map/ppermute | solution.py:172
  40.4 0.0 slice-done
  40.4 0.0 slice-done.2
  40.4 0.0 slice-done.1
  40.4 0.0 slice-done.3
  40.4 1.8 %hidden.1.hidden_ref = bf16[128,1024]{1,0:T(8,128)(2,1)S(1)} custom-call(bf16[128,3072]{1,0:T(8,128)(2,1)S(1)} %bitcast.17, bf16[1,3072,1024]{2,1,0:T(8,128)(2,1)S(1)} %bitcast.10, bf16[1,3072,1024]{2,1,0:T(8,128)(2,1)S(1)} %bitcast.12), custom_call_target="tpu_custom_call" | custom-call | flops 1610612736 | tf_op jit(solution)/shard_map/hidden/pallas_call | solution.py:29
  42.2 0.4 collective-permute-done.rows_ref
  42.6 0.0 slice-done.4
  42.6 0.0 slice-done.5
  42.6 2.7 %expert.1 = bf16[128,3072]{1,0:T(8,128)(2,1)S(1)} custom-call(bf16[128,3072]{1,0:T(8,128)(2,1)S(1)} %collective-permute-done.rows_ref, bf16[1,3072,1024]{2,1,0:T(8,128)(2,1)S(1)} %bitcast.10, bf16[1,3072,1024]{2,1,0:T(8,128)(2,1)S(1)} %bitcast.12, bf16[1,1024,3072]{2,1,0:T(8,128)(2,1)S(1)} %bitcast.14), custom_call_target="tpu_custom_call" | custom-call | flops 2415919104 | tf_op jit(solution)/shard_map/expert/pallas_call | solution.py:29
  45.3 2.1 %collective-permute-start.1 = (bf16[128,3072]{1,0:T(8,128)(2,1)S(1)}, bf16[128,3072]{1,0:T(8,128)(2,1)S(1)}, u32[]{:S(2)}, u32[]{:S(2)}) collective-permute-start(bf16[128,3072]{1,0:T(8,128)(2,1)S(1)} %expert.1), channel_id=1, source_target_pairs={{0,1},{1,0},{2,3},{3,2},{4,5},{5,4},{6,7},{7,6},{8,9},{9,8},{10,11... | collective-permute-start | bytes 2359304 | tf_op jit(solution)/shard_map/ppermute | solution.py:172
  47.4 0.5 weights.1
  47.9 1.0 %down.1 = f32[128,3072]{1,0:T(8,128)S(1)} custom-call(bf16[128,1024]{1,0:T(8,128)(2,1)S(1)} %hidden.1.hidden_ref, bf16[1,1024,3072]{2,1,0:T(8,128)(2,1)S(1)} %bitcast.14), custom_call_target="tpu_custom_call" | custom-call | flops 805306368 | tf_op jit(solution)/shard_map/down/pallas_call | solution.py:29
  48.9 0.6 collective-permute-done.1
  49.5 0.2 fusion
  49.7 17.9 %all_to_all.11 = bf16[16,8,3072]{2,1,0:T(8,128)(2,1)S(1)} all-to-all(bf16[16,8,3072]{2,1,0:T(8,128)(2,1)S(1)} %fusion), channel_id=1, replica_groups=mesh['dp'=8,'x'=4,'zh'=2,'y'=4,'core'=2] {'x','y'}, dimensions={0} | all-to-all | bytes 1572864 | tf_op jit(solution)/shard_map/all_to_all | solution.py:198
  67.6 0.2 mix.1
  67.9 13.5 %all-gather.1 = bf16[16,3072]{1,0:T(8,128)(2,1)S(1)} all-gather(bf16[8,3072]{1,0:T(8,128)(2,1)S(1)} %get-tuple-element.30), channel_id=3, replica_groups=mesh['dp'=8,'x'=4,'zh'=2,'y'=4,'core'=2] {'zh'}, dimensions={0}, use_global_device_ids=true | all-gather | bytes 147456 | tf_op jit(solution)/shard_map/all_gather | solution.py:201
  81.4 0.6 final.1
  (3 shorter events, 0.0 us)
Async XLA Ops:
  0.0 40.4 %slice-start = ((s8[6291456]{0:T(1024)(128)(4,1)}), s8[4194304]{0:T(1024)(128)(4,1)S(1)}, s32[]{:S(2)}) async-start(s8[6291456]{0:T(1024)(128)(4,1)} %bitcast.9), calls=%async_computation.2 | async-start | bytes 8388608
  0.0 40.4 %slice-start.2 = ((s8[6291456]{0:T(1024)(128)(4,1)}), s8[4194304]{0:T(1024)(128)(4,1)S(1)}, s32[]{:S(2)}) async-start(s8[6291456]{0:T(1024)(128)(4,1)} %bitcast.11), calls=%async_computation.4 | async-start | bytes 8388608
  0.0 40.4 %slice-start.1 = ((s8[6291456]{0:T(1024)(128)(4,1)}), s8[2097152]{0:T(1024)(128)(4,1)S(1)}, s32[]{:S(2)}) async-start(s8[6291456]{0:T(1024)(128)(4,1)} %bitcast.9), calls=%async_computation.3 | async-start | bytes 4194304
  0.0 40.4 %slice-start.3 = ((s8[6291456]{0:T(1024)(128)(4,1)}), s8[2097152]{0:T(1024)(128)(4,1)S(1)}, s32[]{:S(2)}) async-start(s8[6291456]{0:T(1024)(128)(4,1)} %bitcast.11), calls=%async_computation.5 | async-start | bytes 4194304
  16.4 26.2 %slice-start.4 = ((s8[6291456]{0:T(1024)(128)(4,1)}), s8[4194304]{0:T(1024)(128)(4,1)S(1)}, s32[]{:S(2)}) async-start(s8[6291456]{0:T(1024)(128)(4,1)} %bitcast.13), calls=%async_computation.6 | async-start | bytes 8388608
  38.3 4.3 %slice-start.5 = ((s8[6291456]{0:T(1024)(128)(4,1)}), s8[2097152]{0:T(1024)(128)(4,1)S(1)}, s32[]{:S(2)}) async-start(s8[6291456]{0:T(1024)(128)(4,1)} %bitcast.13), calls=%async_computation.7 | async-start | bytes 4194304
  38.3 4.3 %collective-permute-start = (bf16[128,3072]{1,0:T(8,128)(2,1)S(1)}, bf16[128,3072]{1,0:T(8,128)(2,1)S(1)}, u32[]{:S(2)}, u32[]{:S(2)}) collective-permute-start(bf16[128,3072]{1,0:T(8,128)(2,1)S(1)} %bitcast.16), channel_id=1, source_target_pairs={{0,1},{1,0},{2,3},{3,2},{4,5},{5,4},{6,7},{7,6},{8,9},{9,8},{10,11... | collective-permute-start | bytes 2359304 | tf_op jit(solution)/shard_map/ppermute | solution.py:172
  45.3 4.2 %collective-permute-start.1 = (bf16[128,3072]{1,0:T(8,128)(2,1)S(1)}, bf16[128,3072]{1,0:T(8,128)(2,1)S(1)}, u32[]{:S(2)}, u32[]{:S(2)}) collective-permute-start(bf16[128,3072]{1,0:T(8,128)(2,1)S(1)} %expert.1), channel_id=1, source_target_pairs={{0,1},{1,0},{2,3},{3,2},{4,5},{5,4},{6,7},{7,6},{8,9},{9,8},{10,11... | collective-permute-start | bytes 2359304 | tf_op jit(solution)/shard_map/ppermute | solution.py:172

commit v9 on v8

--- a/solution.py
+++ b/solution.py
@@ -64,7 +64,6 @@
         out_specs=pl.BlockSpec(memory_space=VMEM),
         scratch_shapes=[pltpu.VMEM((8, META), F32)],
         compiler_params=pltpu.CompilerParams(vmem_limit_bytes=2**20),
-        cost_estimate=pl.CostEstimate(flops=2**35, transcendentals=0, bytes_accessed=0),
         name="pack",
     )(*in_hbm(tokens, ids.T, gate_weights.T))
 
@@ -90,13 +89,13 @@
     slots = dot(jnp.concatenate(places, axis=1), both_ref[...]).astype(BF16)
     for x in range(X):
         for y in range(Y):
-            out_ref[x * Y + y] = slots[x * 2 * SLOTS : (x + 1) * 2 * SLOTS]
+            out_ref[y * X + x] = slots[x * 2 * SLOTS : (x + 1) * 2 * SLOTS]
 
 
 def placed(zh, own, halves):
     width = own.shape[1] - META
     outs = [((X * Y, 2 * SLOTS, width), BF16)]
-    return call(place_kernel, outs, (zh, own, halves), "place", [pltpu.VMEM((16, width), BF16)])[0]
+    return call(place_kernel, outs, (zh, own, halves), "place", [pltpu.VMEM((16, width), BF16)], flops=2**35)[0]
 
 
 BLOCK = 512
@@ -133,7 +132,7 @@
     fields = dot(eye, meta[:, :rows], ((1,), (1,)))
     lanes = X * Y * 2 * SLOTS
     r = iota((rows, lanes), 1)
-    expert = ((r // (Y * 2 * SLOTS)) * ZH + zh).astype(F32)
+    expert = (((r // (2 * SLOTS)) % X) * ZH + zh).astype(F32)
     first = fields[:, 0:1] == expert
     second = fields[:, 1:2] == expert
     named = jnp.where(first | second, 1.0, 0.0)
@@ -181,7 +180,7 @@
     wg, wu, wd = gate_proj, up_proj, down_proj
     slots = placed(zh, own, halves)
     half = slots.shape[0] * slots.shape[1]
-    rows = lax.all_to_all(slots, ("x", "y"), 0, 0, tiled=True).reshape(half, width)
+    rows = lax.all_to_all(slots, ("y", "x"), 0, 0, tiled=True).reshape(half, width)
     core_rows = swapped(rows, "core")
     third = 2 * half * width * units
     hidden = call(hidden_kernel, [((half, units), BF16)], (rows, wg, wu), "hidden", flops=2 * third)[0]
@@ -195,7 +194,7 @@
     mixers = call(weights_kernel, outs, (zh, own, halves), "weights", flops=2**28)
     arrived, part, (own_weights, other_weights) = lax.optimization_barrier((arrived, part, mixers))
     pair = (part + arrived.astype(F32)).astype(BF16).reshape(slots.shape)
-    back = lax.all_to_all(pair, ("x", "y"), 0, 0, tiled=True)
+    back = lax.all_to_all(pair, ("y", "x"), 0, 0, tiled=True)
     outs = [((8, width), F32), ((8, width), BF16)]
     keep, send = call(both_kernel, outs, (own_weights, other_weights, back.reshape(half, width)), "mix")
     gathered = lax.all_gather(send, "zh")

time: 82.2 us -> 81.8 us (level)
  no operation moved by 1% of the time
where the time goes in v9:
time: 81.8 us; the launch traced here: 81.6 us
  blocking collectives  68 us (83%)
  Pallas kernels  8.13 us (10%)
  starting transfers between devices  4.11 us (5%)
  waiting for transfers between devices  0.95 us (1%)
    all_to_all x1, blocking collectives, on_device(): lax.all_to_all(slots, ('y', 'x'), 0, 0, tiled=True).reshape(half, width)  22.1 us
    all_to_all x1, blocking collectives, on_device(): back = lax.all_to_all(pair, ('y', 'x'), 0, 0, tiled=True)  17.6 us
    all_gather x1, blocking collectives, on_device(): halves = lax.all_gather(own, 'zh')  14.9 us
    all_gather x1, blocking collectives, on_device(): gathered = lax.all_gather(send, 'zh')  13.5 us
    pallas_call x6, Pallas kernels, call(): pl.pallas_call(kernel, out_shape=tuple((VMEM(shape, dtype) for shape, dty...  6.67 us
    ppermute x2, starting transfers between devices, swapped(): return lax.ppermute(value, axis, [(0, 1), (1, 0)])  4.11 us
  transfers between devices with their start and end apart: 2, of which 2 were waited for; matrix products, arithmetic and copies ran while one was open for 0% of the time, Pallas kernels for 4%

profile of v9, /device:TPU:192, one launch (start us, length us, event | category | flops | bytes accessed | tf_op | source)
XLA Modules:
  0.0 81.6 jit_solution(2621916355953900932)
XLA Ops:
  0.0 0.8 %pack.1.own_ref = bf16[8,3200]{1,0:T(8,128)(2,1)S(1)} custom-call(bf16[8,3072]{1,0:T(8,128)(2,1)} %tok_ref.1, s32[2,8]{1,0:T(2,128)} %bitcast.21, f32[2,8]{1,0:T(2,128)} %bitcast.22), custom_call_target="tpu_custom_call" | custom-call | tf_op jit(solution)/shard_map/pack/pallas_call | solution.py:61
  0.8 14.9 %all-gather = bf16[16,3200]{1,0:T(8,128)(2,1)S(1)} all-gather(bf16[8,3200]{1,0:T(8,128)(2,1)S(1)} %pack.1.own_ref), channel_id=2, replica_groups=mesh['dp'=8,'x'=4,'zh'=2,'y'=4,'core'=2] {'zh'}, dimensions={0}, use_global_device_ids=true | all-gather | bytes 153600 | tf_op jit(solution)/shard_map/all_gather | solution.py:179
  15.8 0.0 slice-start
  15.8 0.0 slice-start.2
  15.8 0.0 slice-start.1
  15.8 0.0 slice-start.3
  15.8 0.4 place.1
  16.2 0.0 slice-start.4
  16.2 22.1 %all_to_all.10 = bf16[16,8,3072]{2,1,0:T(8,128)(2,1)S(1)} all-to-all(bf16[16,8,3072]{2,1,0:T(8,128)(2,1)S(1)} %place.1), channel_id=1, replica_groups=mesh['dp'=8,'x'=4,'zh'=2,'y'=4,'core'=2] {'y','x'}, dimensions={0} | all-to-all | bytes 1572864 | tf_op jit(solution)/shard_map/all_to_all | solution.py:183
  38.2 0.0 slice-start.5
  38.2 2.0 %collective-permute-start = (bf16[128,3072]{1,0:T(8,128)(2,1)S(1)}, bf16[128,3072]{1,0:T(8,128)(2,1)S(1)}, u32[]{:S(2)}, u32[]{:S(2)}) collective-permute-start(bf16[128,3072]{1,0:T(8,128)(2,1)S(1)} %bitcast.16), channel_id=1, source_target_pairs={{0,1},{1,0},{2,3},{3,2},{4,5},{5,4},{6,7},{7,6},{8,9},{9,8},{10,11... | collective-permute-start | bytes 2359304 | tf_op jit(solution)/shard_map/ppermute | solution.py:171
  40.3 0.0 slice-done
  40.3 0.0 slice-done.2
  40.3 0.0 slice-done.1
  40.3 0.0 slice-done.3
  40.3 1.8 %hidden.1.hidden_ref = bf16[128,1024]{1,0:T(8,128)(2,1)S(1)} custom-call(bf16[128,3072]{1,0:T(8,128)(2,1)S(1)} %bitcast.17, bf16[1,3072,1024]{2,1,0:T(8,128)(2,1)S(1)} %bitcast.10, bf16[1,3072,1024]{2,1,0:T(8,128)(2,1)S(1)} %bitcast.12), custom_call_target="tpu_custom_call" | custom-call | flops 1610612736 | tf_op jit(solution)/shard_map/hidden/pallas_call | solution.py:29
  42.2 0.4 collective-permute-done.rows_ref
  42.5 0.0 slice-done.4
  42.5 0.0 slice-done.5
  42.5 2.7 %expert.1 = bf16[128,3072]{1,0:T(8,128)(2,1)S(1)} custom-call(bf16[128,3072]{1,0:T(8,128)(2,1)S(1)} %collective-permute-done.rows_ref, bf16[1,3072,1024]{2,1,0:T(8,128)(2,1)S(1)} %bitcast.10, bf16[1,3072,1024]{2,1,0:T(8,128)(2,1)S(1)} %bitcast.12, bf16[1,1024,3072]{2,1,0:T(8,128)(2,1)S(1)} %bitcast.14), custom_call_target="tpu_custom_call" | custom-call | flops 2415919104 | tf_op jit(solution)/shard_map/expert/pallas_call | solution.py:29
  45.3 2.1 %collective-permute-start.1 = (bf16[128,3072]{1,0:T(8,128)(2,1)S(1)}, bf16[128,3072]{1,0:T(8,128)(2,1)S(1)}, u32[]{:S(2)}, u32[]{:S(2)}) collective-permute-start(bf16[128,3072]{1,0:T(8,128)(2,1)S(1)} %expert.1), channel_id=1, source_target_pairs={{0,1},{1,0},{2,3},{3,2},{4,5},{5,4},{6,7},{7,6},{8,9},{9,8},{10,11... | collective-permute-start | bytes 2359304 | tf_op jit(solution)/shard_map/ppermute | solution.py:171
  47.3 0.5 weights.1
  47.8 1.0 %down.1 = f32[128,3072]{1,0:T(8,128)S(1)} custom-call(bf16[128,1024]{1,0:T(8,128)(2,1)S(1)} %hidden.1.hidden_ref, bf16[1,1024,3072]{2,1,0:T(8,128)(2,1)S(1)} %bitcast.14), custom_call_target="tpu_custom_call" | custom-call | flops 805306368 | tf_op jit(solution)/shard_map/down/pallas_call | solution.py:29
  48.9 0.6 collective-permute-done.1
  49.4 0.2 fusion
  49.7 17.6 %all_to_all.11 = bf16[16,8,3072]{2,1,0:T(8,128)(2,1)S(1)} all-to-all(bf16[16,8,3072]{2,1,0:T(8,128)(2,1)S(1)} %fusion), channel_id=1, replica_groups=mesh['dp'=8,'x'=4,'zh'=2,'y'=4,'core'=2] {'y','x'}, dimensions={0} | all-to-all | bytes 1572864 | tf_op jit(solution)/shard_map/all_to_all | solution.py:197
  67.2 0.2 mix.1
  67.5 13.5 %all-gather.1 = bf16[16,3072]{1,0:T(8,128)(2,1)S(1)} all-gather(bf16[8,3072]{1,0:T(8,128)(2,1)S(1)} %get-tuple-element.30), channel_id=3, replica_groups=mesh['dp'=8,'x'=4,'zh'=2,'y'=4,'core'=2] {'zh'}, dimensions={0}, use_global_device_ids=true | all-gather | bytes 147456 | tf_op jit(solution)/shard_map/all_gather | solution.py:200
  80.9 0.6 final.1
  (3 shorter events, 0.0 us)
Async XLA Ops:
  15.8 24.5 %slice-start = ((s8[6291456]{0:T(1024)(128)(4,1)}), s8[4194304]{0:T(1024)(128)(4,1)S(1)}, s32[]{:S(2)}) async-start(s8[6291456]{0:T(1024)(128)(4,1)} %bitcast.9), calls=%async_computation.2 | async-start | bytes 8388608
  15.8 24.5 %slice-start.2 = ((s8[6291456]{0:T(1024)(128)(4,1)}), s8[4194304]{0:T(1024)(128)(4,1)S(1)}, s32[]{:S(2)}) async-start(s8[6291456]{0:T(1024)(128)(4,1)} %bitcast.11), calls=%async_computation.4 | async-start | bytes 8388608
  15.8 24.5 %slice-start.1 = ((s8[6291456]{0:T(1024)(128)(4,1)}), s8[2097152]{0:T(1024)(128)(4,1)S(1)}, s32[]{:S(2)}) async-start(s8[6291456]{0:T(1024)(128)(4,1)} %bitcast.9), calls=%async_computation.3 | async-start | bytes 4194304
  15.8 24.6 %slice-start.3 = ((s8[6291456]{0:T(1024)(128)(4,1)}), s8[2097152]{0:T(1024)(128)(4,1)S(1)}, s32[]{:S(2)}) async-start(s8[6291456]{0:T(1024)(128)(4,1)} %bitcast.11), calls=%async_computation.5 | async-start | bytes 4194304
  16.2 26.4 %slice-start.4 = ((s8[6291456]{0:T(1024)(128)(4,1)}), s8[4194304]{0:T(1024)(128)(4,1)S(1)}, s32[]{:S(2)}) async-start(s8[6291456]{0:T(1024)(128)(4,1)} %bitcast.13), calls=%async_computation.6 | async-start | bytes 8388608
  38.2 4.3 %slice-start.5 = ((s8[6291456]{0:T(1024)(128)(4,1)}), s8[2097152]{0:T(1024)(128)(4,1)S(1)}, s32[]{:S(2)}) async-start(s8[6291456]{0:T(1024)(128)(4,1)} %bitcast.13), calls=%async_computation.7 | async-start | bytes 4194304
  38.2 4.3 %collective-permute-start = (bf16[128,3072]{1,0:T(8,128)(2,1)S(1)}, bf16[128,3072]{1,0:T(8,128)(2,1)S(1)}, u32[]{:S(2)}, u32[]{:S(2)}) collective-permute-start(bf16[128,3072]{1,0:T(8,128)(2,1)S(1)} %bitcast.16), channel_id=1, source_target_pairs={{0,1},{1,0},{2,3},{3,2},{4,5},{5,4},{6,7},{7,6},{8,9},{9,8},{10,11... | collective-permute-start | bytes 2359304 | tf_op jit(solution)/shard_map/ppermute | solution.py:171
  45.3 4.2 %collective-permute-start.1 = (bf16[128,3072]{1,0:T(8,128)(2,1)S(1)}, bf16[128,3072]{1,0:T(8,128)(2,1)S(1)}, u32[]{:S(2)}, u32[]{:S(2)}) collective-permute-start(bf16[128,3072]{1,0:T(8,128)(2,1)S(1)} %expert.1), channel_id=1, source_target_pairs={{0,1},{1,0},{2,3},{3,2},{4,5},{5,4},{6,7},{7,6},{8,9},{9,8},{10,11... | collective-permute-start | bytes 2359304 | tf_op jit(solution)/shard_map/ppermute | solution.py:171

commit v10 on v8

--- a/solution.py
+++ b/solution.py
@@ -64,7 +64,6 @@
         out_specs=pl.BlockSpec(memory_space=VMEM),
         scratch_shapes=[pltpu.VMEM((8, META), F32)],
         compiler_params=pltpu.CompilerParams(vmem_limit_bytes=2**20),
-        cost_estimate=pl.CostEstimate(flops=2**35, transcendentals=0, bytes_accessed=0),
         name="pack",
     )(*in_hbm(tokens, ids.T, gate_weights.T))
 
@@ -96,7 +95,7 @@
 def placed(zh, own, halves):
     width = own.shape[1] - META
     outs = [((X * Y, 2 * SLOTS, width), BF16)]
-    return call(place_kernel, outs, (zh, own, halves), "place", [pltpu.VMEM((16, width), BF16)])[0]
+    return call(place_kernel, outs, (zh, own, halves), "place", [pltpu.VMEM((16, width), BF16)], flops=2**35)[0]
 
 
 BLOCK = 512
@@ -162,10 +161,6 @@
     total = dot(jnp.concatenate([own_ref[...], other_ref[...]], axis=0), rows_ref[...])
     keep_ref[...] = total[0:8] + total[8:16] + total[16:24]
     send_ref[...] = (total[24:32] + total[32:40] + total[40:48]).astype(BF16)
-
-
-def final_kernel(zh_ref, keep_ref, gathered_ref, out_ref):
-    out_ref[...] = (keep_ref[...] + gathered_ref[1 - zh_ref[0]].astype(F32)).astype(BF16)
 
 
 def swapped(value, axis):
@@ -199,14 +194,8 @@
     outs = [((8, width), F32), ((8, width), BF16)]
     keep, send = call(both_kernel, outs, (own_weights, other_weights, back.reshape(half, width)), "mix")
     gathered = lax.all_gather(send, "zh")
-    return pl.pallas_call(
-        final_kernel,
-        out_shape=jax.ShapeDtypeStruct((8, width), BF16),
-        in_specs=[pl.BlockSpec(memory_space=SMEM), pl.BlockSpec(memory_space=VMEM), pl.BlockSpec(memory_space=VMEM)],
-        out_specs=pl.BlockSpec(memory_space=VMEM),
-        compiler_params=pltpu.CompilerParams(vmem_limit_bytes=2**20),
-        name="final",
-    )(zh, pltpu.with_memory_space_constraint(keep, VMEM), pltpu.with_memory_space_constraint(gathered, VMEM))
+    arriving = jnp.where(zh[0] == 0, gathered[1], gathered[0])
+    return (keep + arriving.astype(F32)).astype(BF16)
 
 
 def solution(mesh):

time: 82.2 us -> 83.7 us (1.018)
  blocking collectives: 68.3 us -> 50.3 us
  waiting for transfers between devices: 0.96 us -> 16 us
  starting transfers between devices: 4.09 us -> 7.77 us
  other arithmetic: 0.19 us -> 1.7 us
    all_to_all x1 -> x0, blocking collectives: 17.9 us -> none  [on_device(): back = lax.all_to_all(pair, ('x', 'y'), 0, 0, tiled=True)]
    all_to_all x0 -> x1, waiting for transfers between devices: none -> 15.1 us  [on_device(): back = lax.all_to_all(pair, ('x', 'y'), 0, 0, tiled=True)]
    all_to_all x0 -> x1, starting transfers between devices: none -> 3.67 us  [on_device(): back = lax.all_to_all(pair, ('x', 'y'), 0, 0, tiled=True)]
    reshape x1, other arithmetic: 0.18 us -> 1.06 us  [on_device(): pair = (part + arrived.astype(F32)).astype(BF16).reshape(slots.shape)]
  transfers between devices with their start and end apart: 2 -> 3, of which waited for: 2 -> 3; matrix products, arithmetic and copies ran while one was open for 0% -> 0% of each run, Pallas kernels for 4% -> 4%
where the time goes in v10:
time: 83.7 us; the launch traced here: 83.4 us
  blocking collectives  50.3 us (60%)
  waiting for transfers between devices  16 us (19%)
  starting transfers between devices  7.77 us (9%)
  Pallas kernels  7.5 us (9%)
  other arithmetic  1.7 us (2%)
    all_to_all x1, blocking collectives, on_device(): lax.all_to_all(slots, ('x', 'y'), 0, 0, tiled=True).reshape(half, width)  21.8 us
    all_to_all x1, waiting for transfers between devices, on_device(): back = lax.all_to_all(pair, ('x', 'y'), 0, 0, tiled=True)  15.1 us
    all_gather x1, blocking collectives, on_device(): halves = lax.all_gather(own, 'zh')  14.9 us
    all_gather x1, blocking collectives, on_device(): gathered = lax.all_gather(send, 'zh')  13.5 us
    pallas_call x6, Pallas kernels, call(): pl.pallas_call(kernel, out_shape=tuple((VMEM(shape, dtype) for shape, dty...  6.67 us
    ppermute x2, starting transfers between devices, swapped(): return lax.ppermute(value, axis, [(0, 1), (1, 0)])  4.1 us
    all_to_all x1, starting transfers between devices, on_device(): back = lax.all_to_all(pair, ('x', 'y'), 0, 0, tiled=True)  3.67 us
  transfers between devices with their start and end apart: 3, of which 3 were waited for; matrix products, arithmetic and copies ran while one was open for 0% of the time, Pallas kernels for 4%

profile of v10, /device:TPU:192, one launch (start us, length us, event | category | flops | bytes accessed | tf_op | source)
XLA Modules:
  0.0 83.4 jit_solution(15367843085388228046)
XLA Ops:
  0.0 0.8 pack.1.own_ref
  0.8 14.9 %all-gather = bf16[16,3200]{1,0:T(8,128)(2,1)S(1)} all-gather(bf16[8,3200]{1,0:T(8,128)(2,1)S(1)} %pack.1.own_ref), channel_id=2, replica_groups=mesh['dp'=8,'x'=4,'zh'=2,'y'=4,'core'=2] {'zh'}, dimensions={0}, use_global_device_ids=true | all-gather | bytes 153600 | tf_op jit(solution)/shard_map/all_gather | solution.py:175
  15.8 0.0 slice-start
  15.8 0.0 slice-start.2
  15.8 0.0 slice-start.1
  15.8 0.0 slice-start.3
  15.8 0.4 place.1
  16.2 0.0 slice-start.4
  16.2 21.8 %all_to_all.10 = bf16[16,8,3072]{2,1,0:T(8,128)(2,1)S(1)} all-to-all(bf16[16,8,3072]{2,1,0:T(8,128)(2,1)S(1)} %place.1), channel_id=1, replica_groups=mesh['dp'=8,'x'=4,'zh'=2,'y'=4,'core'=2] {'x','y'}, dimensions={0} | all-to-all | bytes 1572864 | tf_op jit(solution)/shard_map/all_to_all | solution.py:179
  38.0 0.0 slice-start.5
  38.0 2.0 %collective-permute-start = (bf16[128,3072]{1,0:T(8,128)(2,1)S(1)}, bf16[128,3072]{1,0:T(8,128)(2,1)S(1)}, u32[]{:S(2)}, u32[]{:S(2)}) collective-permute-start(bf16[128,3072]{1,0:T(8,128)(2,1)S(1)} %bitcast.15), channel_id=1, source_target_pairs={{0,1},{1,0},{2,3},{3,2},{4,5},{5,4},{6,7},{7,6},{8,9},{9,8},{10,11... | collective-permute-start | bytes 2359304 | tf_op jit(solution)/shard_map/ppermute | solution.py:167
  40.1 0.0 slice-done
  40.1 0.0 slice-done.2
  40.1 0.0 slice-done.1
  40.1 0.0 slice-done.3
  40.1 1.8 %hidden.1.hidden_ref = bf16[128,1024]{1,0:T(8,128)(2,1)S(1)} custom-call(bf16[128,3072]{1,0:T(8,128)(2,1)S(1)} %bitcast.16, bf16[1,3072,1024]{2,1,0:T(8,128)(2,1)S(1)} %bitcast.9, bf16[1,3072,1024]{2,1,0:T(8,128)(2,1)S(1)} %bitcast.11), custom_call_target="tpu_custom_call" | custom-call | flops 1610612736 | tf_op jit(solution)/shard_map/hidden/pallas_call | solution.py:29
  41.9 0.4 collective-permute-done.rows_ref
  42.3 0.0 slice-done.4
  42.3 0.0 slice-done.5
  42.3 2.7 %expert.1 = bf16[128,3072]{1,0:T(8,128)(2,1)S(1)} custom-call(bf16[128,3072]{1,0:T(8,128)(2,1)S(1)} %collective-permute-done.rows_ref, bf16[1,3072,1024]{2,1,0:T(8,128)(2,1)S(1)} %bitcast.9, bf16[1,3072,1024]{2,1,0:T(8,128)(2,1)S(1)} %bitcast.11, bf16[1,1024,3072]{2,1,0:T(8,128)(2,1)S(1)} %bitcast.13), custom_call_target="tpu_custom_call" | custom-call | flops 2415919104 | tf_op jit(solution)/shard_map/expert/pallas_call | solution.py:29
  45.0 2.1 %collective-permute-start.1 = (bf16[128,3072]{1,0:T(8,128)(2,1)S(1)}, bf16[128,3072]{1,0:T(8,128)(2,1)S(1)}, u32[]{:S(2)}, u32[]{:S(2)}) collective-permute-start(bf16[128,3072]{1,0:T(8,128)(2,1)S(1)} %expert.1), channel_id=1, source_target_pairs={{0,1},{1,0},{2,3},{3,2},{4,5},{5,4},{6,7},{7,6},{8,9},{9,8},{10,11... | collective-permute-start | bytes 2359304 | tf_op jit(solution)/shard_map/ppermute | solution.py:167
  47.1 0.5 weights.1
  47.6 1.0 %down.1 = f32[128,3072]{1,0:T(8,128)S(1)} custom-call(bf16[128,1024]{1,0:T(8,128)(2,1)S(1)} %hidden.1.hidden_ref, bf16[1,1024,3072]{2,1,0:T(8,128)(2,1)S(1)} %bitcast.13), custom_call_target="tpu_custom_call" | custom-call | flops 805306368 | tf_op jit(solution)/shard_map/down/pallas_call | solution.py:29
  48.6 0.6 collective-permute-done.1
  49.2 1.1 %fusion = bf16[16,8,3072]{2,1,0:T(8,128)(2,1)} fusion(f32[128,3072]{1,0:T(8,128)S(1)} %down.1, bf16[128,3072]{1,0:T(8,128)(2,1)S(1)} %collective-permute-done.1), kind=kLoop, calls=%fused_computation.1 | loop fusion | flops 1179648 | bytes 3145728 | tf_op jit(solution)/shard_map/reshape | solution.py:192
  50.3 3.7 %all-to-all-start.1 = ((bf16[16,8,3072]{2,1,0:T(8,128)(2,1)}), bf16[16,8,3072]{2,1,0:T(8,128)(2,1)S(1)}, u32[]{:S(2)}, u32[]{:S(2)}) async-start(bf16[16,8,3072]{2,1,0:T(8,128)(2,1)} %fusion), calls=%async_computation.1 | async-start | bytes 1572864 | tf_op jit(solution)/shard_map/all_to_all | solution.py:193
  54.0 15.1 %all-to-all-done.1 = bf16[16,8,3072]{2,1,0:T(8,128)(2,1)S(1)} async-done(((bf16[16,8,3072]{2,1,0:T(8,128)(2,1)}), bf16[16,8,3072]{2,1,0:T(8,128)(2,1)S(1)}, u32[]{:S(2)}, u32[]{:S(2)}) %all-to-all-start.1) | async-done | bytes 786464 | tf_op jit(solution)/shard_map/all_to_all | solution.py:193
  69.1 0.2 mix.1
  69.3 13.5 %all-gather.1 = bf16[16,3072]{1,0:T(8,128)(2,1)S(1)} all-gather(bf16[8,3072]{1,0:T(8,128)(2,1)S(1)} %get-tuple-element.30), channel_id=3, replica_groups=mesh['dp'=8,'x'=4,'zh'=2,'y'=4,'core'=2] {'zh'}, dimensions={0}, use_global_device_ids=true | all-gather | bytes 147456 | tf_op jit(solution)/shard_map/all_gather | solution.py:196
  82.8 0.6 fusion.1
  (3 shorter events, 0.0 us)
Async XLA Ops:
  15.8 24.3 %slice-start = ((s8[6291456]{0:T(1024)(128)(4,1)}), s8[4194304]{0:T(1024)(128)(4,1)S(1)}, s32[]{:S(2)}) async-start(s8[6291456]{0:T(1024)(128)(4,1)} %bitcast.8), calls=%async_computation.2 | async-start | bytes 8388608
  15.8 24.3 %slice-start.2 = ((s8[6291456]{0:T(1024)(128)(4,1)}), s8[4194304]{0:T(1024)(128)(4,1)S(1)}, s32[]{:S(2)}) async-start(s8[6291456]{0:T(1024)(128)(4,1)} %bitcast.10), calls=%async_computation.4 | async-start | bytes 8388608
  15.8 24.3 %slice-start.1 = ((s8[6291456]{0:T(1024)(128)(4,1)}), s8[2097152]{0:T(1024)(128)(4,1)S(1)}, s32[]{:S(2)}) async-start(s8[6291456]{0:T(1024)(128)(4,1)} %bitcast.8), calls=%async_computation.3 | async-start | bytes 4194304
  15.8 24.3 %slice-start.3 = ((s8[6291456]{0:T(1024)(128)(4,1)}), s8[2097152]{0:T(1024)(128)(4,1)S(1)}, s32[]{:S(2)}) async-start(s8[6291456]{0:T(1024)(128)(4,1)} %bitcast.10), calls=%async_computation.5 | async-start | bytes 4194304
  16.2 26.2 %slice-start.4 = ((s8[6291456]{0:T(1024)(128)(4,1)}), s8[4194304]{0:T(1024)(128)(4,1)S(1)}, s32[]{:S(2)}) async-start(s8[6291456]{0:T(1024)(128)(4,1)} %bitcast.12), calls=%async_computation.6 | async-start | bytes 8388608
  38.0 4.3 %slice-start.5 = ((s8[6291456]{0:T(1024)(128)(4,1)}), s8[2097152]{0:T(1024)(128)(4,1)S(1)}, s32[]{:S(2)}) async-start(s8[6291456]{0:T(1024)(128)(4,1)} %bitcast.12), calls=%async_computation.7 | async-start | bytes 4194304
  38.0 4.3 %collective-permute-start = (bf16[128,3072]{1,0:T(8,128)(2,1)S(1)}, bf16[128,3072]{1,0:T(8,128)(2,1)S(1)}, u32[]{:S(2)}, u32[]{:S(2)}) collective-permute-start(bf16[128,3072]{1,0:T(8,128)(2,1)S(1)} %bitcast.15), channel_id=1, source_target_pairs={{0,1},{1,0},{2,3},{3,2},{4,5},{5,4},{6,7},{7,6},{8,9},{9,8},{10,11... | collective-permute-start | bytes 2359304 | tf_op jit(solution)/shard_map/ppermute | solution.py:167
  45.0 4.2 %collective-permute-start.1 = (bf16[128,3072]{1,0:T(8,128)(2,1)S(1)}, bf16[128,3072]{1,0:T(8,128)(2,1)S(1)}, u32[]{:S(2)}, u32[]{:S(2)}) collective-permute-start(bf16[128,3072]{1,0:T(8,128)(2,1)S(1)} %expert.1), channel_id=1, source_target_pairs={{0,1},{1,0},{2,3},{3,2},{4,5},{5,4},{6,7},{7,6},{8,9},{9,8},{10,11... | collective-permute-start | bytes 2359304 | tf_op jit(solution)/shard_map/ppermute | solution.py:167
  50.3 18.8 %all-to-all-start.1 = ((bf16[16,8,3072]{2,1,0:T(8,128)(2,1)}), bf16[16,8,3072]{2,1,0:T(8,128)(2,1)S(1)}, u32[]{:S(2)}, u32[]{:S(2)}) async-start(bf16[16,8,3072]{2,1,0:T(8,128)(2,1)} %fusion), calls=%async_computation.1 | async-start | bytes 1572864 | tf_op jit(solution)/shard_map/all_to_all | solution.py:193
